TPU v7x, 1024 devices: a whole 4x8x16 slice. The times are simulated.
1024 devices in a mesh: ctx: 128 (over z, y_hi, core), dp: 8 (over x, y_lo).
Axes of the slice: x: 4, y: 8 (y_hi: 4, y_lo: 2; y = y_hi * 2 + y_lo), z: 16, core: 2. Of those that a mesh axis runs over, the one named last changes fastest.
Arguments:
- stream: bfloat16 [3, 16384, 8192], P(None, 'ctx', 'dp'), may hold values from -6 to 6
- short_taps: float32 [3, 3, 8192], replicated, may hold values from -3.5 to 3.5
- decay_rate: float32 [16, 512], P('dp'), may hold values from 1.2207031e-05 to 0.1
- residue: float32 [16, 512], P('dp'), may hold values from -0.4472136 to 0.4472136
Outputs:
- gated_output: bfloat16 [16384, 8192], P('ctx', 'dp')
All inputs are finite; a program needn't handle non-finite values.
Results may differ from a plain program's by a relative error of at most 0.002.
Values may be sent and summed in bfloat16 or wider, within the bound.
No kernel may reach another device: no remote copies, remote signals or barrier semaphores. Data moves between devices by JAX's collectives and lax.ppermute only.
A program may use at most 128 MiB of HBM per device.

v0:
```python
import math

import jax
import jax.numpy as jnp
from jax import lax
from jax.sharding import PartitionSpec as P

GROUP = 16
ORDER = 16


def from_behind(block, axis, distance):
    devices = range(lax.axis_size(axis))
    route = [(i - distance, i) for i in devices if i - distance in devices]
    return lax.ppermute(block, axis, route)


def unfold_taps(seq_taps):
    group_count, length = seq_taps.shape
    padded = jnp.concatenate([seq_taps, jnp.zeros((group_count, length + 1), seq_taps.dtype)], 1)
    tiled = jnp.tile(padded, (1, length))[:, : 2 * length * length]
    return tiled.reshape(group_count, length, 2 * length)[:, :, :length]


def shards(stream, short_taps, decay_rate, residue):
    row_count = stream.shape[1]
    chan_count = stream.shape[2]
    local_groups = chan_count // GROUP
    reach = short_taps.shape[1] - 1
    earlier_rows = from_behind(stream[:, row_count - reach :, :], "ctx", 1)
    extended = jnp.concatenate([earlier_rows, stream], 1)
    dp_index = lax.axis_index("dp")
    local_taps = lax.dynamic_slice_in_dim(short_taps, dp_index * chan_count, chan_count, 2)
    features = local_taps[:, 0, None, :] * extended[:, reach:, :].astype(jnp.float32)
    for lag in range(1, reach + 1):
        features = features + local_taps[:, lag, None, :] * extended[
            :, reach - lag : reach - lag + row_count, :
        ].astype(jnp.float32)
    query = features[0]
    product = features[1] * features[2]
    rate_local, residue_local = (
        lax.all_to_all(decay_rate, "dp", split_axis=1, concat_axis=0, tiled=True),
        lax.all_to_all(residue, "dp", split_axis=1, concat_axis=0, tiled=True),
    )
    block = math.gcd(row_count, 128)
    sub_count = row_count // block
    inner_pos = jnp.arange(block, dtype=jnp.float32)
    powers = jnp.exp(-rate_local[:, :, None] * inner_pos)
    seq_taps = jnp.sum(residue_local[:, :, None] * powers, 0)
    toeplitz = unfold_taps(seq_taps)
    close_inner = jnp.exp(-rate_local[:, :, None] * (block - 1.0 - inner_pos))
    open_inner = residue_local[:, :, None] * jnp.exp(-rate_local[:, :, None] * (inner_pos + 1.0))
    span_inner = jnp.exp(-rate_local * block)
    sub_blocks = product.reshape(sub_count, block, local_groups, GROUP)

    def advance(state, piece):
        inside = jnp.einsum("gst,sgc->tgc", toeplitz, piece, precision=lax.Precision.HIGHEST)
        carried = jnp.einsum("rgt,rgc->tgc", open_inner, state, precision=lax.Precision.HIGHEST)
        fresh = jnp.einsum("rgs,sgc->rgc", close_inner, piece, precision=lax.Precision.HIGHEST)
        return (span_inner[:, :, None] * state + fresh, inside + carried)

    start_state = jnp.zeros((ORDER, local_groups, GROUP), jnp.float32)
    unused_state, local_part = lax.scan(advance, start_state, sub_blocks)
    local_part = local_part.reshape(row_count, local_groups, GROUP)
    grouped = product.reshape(row_count, local_groups, GROUP)
    position = jnp.arange(row_count, dtype=jnp.float32)
    closing = jnp.exp(-rate_local[:, :, None] * (row_count - 1.0 - position))
    end_state = jnp.einsum(
        "rgs,sgc->rgc", closing, grouped, precision=lax.Precision.HIGHEST
    ).reshape(ORDER, chan_count)
    ctx_index = lax.axis_index("ctx")
    piece = lax.all_gather(end_state[None], "ctx", axis=0, tiled=True)
    count = piece.shape[0]
    distance = (ctx_index - 1 - jnp.arange(count, dtype=jnp.int32)).astype(jnp.float32)
    live_mask = (distance >= 0.0).astype(jnp.float32)
    weight = (
        jnp.exp(-rate_local[None] * row_count * jnp.maximum(distance, 0.0)[:, None, None])
        * live_mask[:, None, None]
    )
    summed = jnp.einsum(
        "krg,krgc->rgc",
        weight,
        piece.reshape(count, ORDER, local_groups, GROUP),
        precision=lax.Precision.HIGHEST,
    )
    incoming = summed.reshape(ORDER, chan_count)
    opening = residue_local[:, :, None] * jnp.exp(-rate_local[:, :, None] * (position + 1.0))
    tail_part = jnp.einsum(
        "rgt,rgc->tgc",
        opening,
        incoming.reshape(ORDER, local_groups, GROUP),
        precision=lax.Precision.HIGHEST,
    )
    convolved = (local_part + tail_part).reshape(row_count, chan_count)
    return (query * convolved).astype(jnp.bfloat16)


def solution(mesh):
    in_specs = (P(None, "ctx", "dp"), P(), P("dp", None), P("dp", None))
    out_specs = P("ctx", "dp")
    return jax.shard_map(shards, mesh=mesh, in_specs=in_specs, out_specs=out_specs, check_vma=False)
```

profile of v0, /device:TPU:9, one launch (start us, length us, event | category | flops | bytes accessed | tf_op | source)
XLA Modules:
  0.0 220.5 jit_solution(11231725147214502750)
XLA Ops:
  6.5 0.8 slice.35
  7.4 4.8 %collective-permute-start = (bf16[3,2,1024]{2,1,0:T(2,128)(2,1)S(1)}, bf16[3,2,1024]{2,1,0:T(2,128)(2,1)S(1)}, u32[]{:S(2)}, u32[]{:S(2)}) collective-permute-start(bf16[3,2,1024]{2,1,0:T(2,128)(2,1)S(1)} %slice.35), channel_id=1, source_target_pairs={{0,8},{8,16},{16,24},{24,32},{32,40},{40,48},{48,56},{56,64},{64,7... | collective-permute-start | bytes 36872 | tf_op jit(solution)/shard_map/ppermute | solution.py:15
  12.1 0.8 all_to_all.25
  12.9 0.7 reshape.73
  13.6 5.2 %all-to-all-start.1 = ((f32[8,1,128]{2,1,0:T(1,128)}), f32[8,1,128]{2,1,0:T(1,128)S(1)}, u32[]{:S(2)}, u32[]{:S(2)}) async-start(f32[8,1,128]{2,1,0:T(1,128)} %reshape.73), calls=%async_computation.1 | async-start | bytes 8192 | tf_op jit(solution)/shard_map/all_to_all | solution.py:42
  18.8 0.0 all-gather.2.cloned.1.call-start
  18.8 1.0 constant_dynamic-slice_fusion.1
  19.8 1.5 copy.26
  21.4 1.2 all-to-all-done.1
  22.6 0.5 broadcast.50
  23.1 0.6 reduce.2
  23.8 0.1 reshape.74
  23.8 0.1 copy.32
  23.9 0.0 collective-permute-done
  23.9 0.4 copy.27
  24.3 2.2 multiply_add_fusion
  26.5 0.0 copy-start.1
  26.5 0.1 slice_multiply_fusion
  26.6 1.0 fusion.9
  27.6 0.8 copy.33
  28.4 0.0 all-gather.2.cloned.1.call-update
  28.4 0.0 copy-done.1
  28.5 0.1 all_to_all.22
  28.5 0.7 reshape.75
  29.2 4.4 %all-to-all-start = ((f32[8,1,128]{2,1,0:T(1,128)}), f32[8,1,128]{2,1,0:T(1,128)S(1)}, u32[]{:S(2)}, u32[]{:S(2)}) async-start(f32[8,1,128]{2,1,0:T(1,128)} %reshape.75), calls=%async_computation | async-start | bytes 8192 | tf_op jit(solution)/shard_map/all_to_all | solution.py:43
  33.6 3.8 %all-to-all-done = f32[8,1,128]{2,1,0:T(1,128)S(1)} async-done(((f32[8,1,128]{2,1,0:T(1,128)}), f32[8,1,128]{2,1,0:T(1,128)S(1)}, u32[]{:S(2)}, u32[]{:S(2)}) %all-to-all-start) | async-done | bytes 4128 | tf_op jit(solution)/shard_map/all_to_all | solution.py:43
  37.5 0.6 reduce.3
  38.1 0.1 reshape.76
  38.2 0.1 copy.30
  38.3 0.3 multiply_reduce_fusion.1
  38.7 5.4 %tile.4 = f32[64,128,257]{2,1,0:T(8,128)} broadcast(f32[64,257]{1,0:T(8,128)S(1)} %concatenate.7), dimensions={0,2} | broadcast | bytes 8487168 | tf_op jit(solution)/shard_map/tile | solution.py:21
  44.0 12.2 %tile.10 = f32[64,32896]{1,0:T(8,128)} reshape(f32[64,128,257]{2,1,0:T(8,128)} %tile.4) | data formatting | bytes 16842752 | tf_op jit(solution)/shard_map/tile | solution.py:21
  56.2 0.0 slice-start
  56.2 3.4 %slice-done = f32[64,32768]{1,0:T(8,128)S(1)} async-done(((f32[64,32896]{1,0:T(8,128)}), f32[64,32768]{1,0:T(8,128)S(1)}, s32[]{:S(2)}) %slice-start) | async-done | bytes 8388632 | tf_op jit(solution)/shard_map/slice | solution.py:21
  59.6 5.7 %copy.49 = f32[8,8,128,256]{3,2,1,0:T(8,128)} copy(f32[8,8,128,256]{3,1,2,0:T(8,128)S(1)} %bitcast.46) | data formatting | bytes 16777216
  65.3 0.3 multiply_bitcast_fusion
  65.7 1.3 copy.47
  66.9 0.8 fusion.12
  67.7 5.3 %fusion.2 = f32[64,16,128]{2,1,0:T(8,128)S(1)} fusion(f32[64,16,128]{2,1,0:T(8,128)S(1)} %fusion.12, f32[128,64,16]{0,2,1:T(8,128)S(1)} %bitcast.50, f32[64,128,256]{2,1,0:T(8,128)} %bitcast.48), kind=kOutput, calls=%fused_computation.6 | convolution fusion | flops 201457664 | bytes 5767168 | tf_op jit(solution)/shard_map/while/body/eval_jaxpr/gst,sgc->tgc/dot_general | solution.py:57
  73.1 0.0 copy-start
  73.1 123.8 %all-gather.2.cloned.1.call-done = f32[128,16,1024]{2,1,0:T(8,128)} async-done(((f32[1,16,1024]{2,1,0:T(8,128)}), f32[128,16,1024]{2,1,0:T(8,128)}) %all-gather.2.cloned.1.call-update) | async-done | bytes 8388624 | tf_op jit(solution)/shard_map/all_gather | solution.py:72
  196.9 8.7 %copy.43 = f32[128,16,1024]{0,2,1:T(8,128)} copy(f32[128,16,1024]{2,1,0:T(8,128)} %all-gather.2.cloned.1.call-done) | data formatting | bytes 16777216
  205.6 0.0 copy-done
  205.6 5.6 %multiply_reduce_fusion = f32[16,64,16]{2,1,0:T(8,128)S(1)} fusion(f32[16,64,128,16]{2,3,1,0:T(8,128)} %bitcast.47, f32[16,64,128]{2,1,0:T(8,128)S(1)} %copy-done), kind=kLoop, calls=%fused_computation | loop fusion | flops 4177920 | bytes 8978432
  211.2 1.5 convolution_add_fusion
  212.8 0.1 fusion.7
  212.8 0.9 copy.35
  (11 shorter events, 0.1 us)
Async XLA Ops:
  7.4 16.6 %collective-permute-start = (bf16[3,2,1024]{2,1,0:T(2,128)(2,1)S(1)}, bf16[3,2,1024]{2,1,0:T(2,128)(2,1)S(1)}, u32[]{:S(2)}, u32[]{:S(2)}) collective-permute-start(bf16[3,2,1024]{2,1,0:T(2,128)(2,1)S(1)} %slice.35), channel_id=1, source_target_pairs={{0,8},{8,16},{16,24},{24,32},{32,40},{40,48},{48,56},{56,64},{64,7... | collective-permute-start | bytes 36872 | tf_op jit(solution)/shard_map/ppermute | solution.py:15
  13.6 9.0 %all-to-all-start.1 = ((f32[8,1,128]{2,1,0:T(1,128)}), f32[8,1,128]{2,1,0:T(1,128)S(1)}, u32[]{:S(2)}, u32[]{:S(2)}) async-start(f32[8,1,128]{2,1,0:T(1,128)} %reshape.73), calls=%async_computation.1 | async-start | bytes 8192 | tf_op jit(solution)/shard_map/all_to_all | solution.py:42
  18.8 178.1 %all-gather.2.cloned.1.call-start = ((), (), s32[]{:S(2)}) async-start(), calls=%async_computation.2 | async-start | bytes 8454144 | tf_op jit(solution)/shard_map/all_gather | solution.py:72
  26.5 1.9 copy-start.1
  29.2 8.3 %all-to-all-start = ((f32[8,1,128]{2,1,0:T(1,128)}), f32[8,1,128]{2,1,0:T(1,128)S(1)}, u32[]{:S(2)}, u32[]{:S(2)}) async-start(f32[8,1,128]{2,1,0:T(1,128)} %reshape.75), calls=%async_computation | async-start | bytes 8192 | tf_op jit(solution)/shard_map/all_to_all | solution.py:43
  56.2 3.4 %slice-start = ((f32[64,32896]{1,0:T(8,128)}), f32[64,32768]{1,0:T(8,128)S(1)}, s32[]{:S(2)}) async-start(f32[64,32896]{1,0:T(8,128)} %tile.10), calls=%async_computation.3 | async-start | bytes 16777216 | tf_op jit(solution)/shard_map/slice | solution.py:21
  73.1 132.5 %copy-start = (f32[16,64,128]{2,1,0:T(8,128)S(1)}, f32[16,64,128]{2,1,0:T(8,128)}, u32[]{:S(2)}) copy-start(f32[16,64,128]{2,1,0:T(8,128)} %copy.47) | copy-start | bytes 1572868
Sparse Core Ops, SparseCore 0:
  28.6 168.2 all-gather.1
where the time goes:
time: 221 us
  waiting for transfers between devices  129 us (58%)
  local copies, waits for them, and re-layouts  45.2 us (20%)
  starting transfers between devices  14.4 us (7%)
  between operations  13.6 us (6%)
  other arithmetic  9.89 us (4%)
  matrix products  8.66 us (4%)
    all_gather x1, waiting for transfers between devices, shards(): piece = lax.all_gather(end_state[None], 'ctx', axis=0, tiled=True)  124 us
    unnamed x14, local copies, waits for them, and re-layouts  18.8 us
    another operation x2, local copies, waits for them, and re-layouts, unfold_taps(): tiled = jnp.tile(padded, (1, length))[:, :2 * length * length]  17.6 us
    unnamed x2, other arithmetic  5.98 us
    dot_general x1, matrix products, advance(): jnp.einsum('gst,sgc->tgc', toeplitz, piece, precision=lax.Precision.HIGHEST)  5.31 us
    all_to_all x1, starting transfers between devices, shards(): lax.all_to_all(decay_rate, 'dp', split_axis=1, concat_axis=0, tiled=True)  5.2 us
    ppermute x1, starting transfers between devices, from_behind(): return lax.ppermute(block, axis, route)  4.78 us
  transfers between devices with their start and end apart: 4, of which 3 were waited for; matrix products, arithmetic and copies ran while one was open for 17% of the time, Pallas kernels for 0%

commit v1 on v0

v1 whole, which is shorter than its diff:
```python
import functools

import jax
import jax.numpy as jnp
from jax import lax
from jax.experimental import pallas as pl
from jax.experimental.pallas import tpu as pltpu
from jax.sharding import PartitionSpec as P


GROUP = 16
ORDER = 16
TAPS = 3
CUTS = 2
RUNS = 8
JUMPS = (1, 4, 3, 2)
LANES = 128
SUB = 8
F32 = jnp.float32


def low_half(shape):
    return lax.broadcasted_iota(jnp.int32, shape, len(shape) - 1) < LANES // 2


def pick(mask, low, high):
    return jnp.where(mask, low, high)


def half_turn(x):
    return pltpu.roll(x, LANES // 2, x.ndim - 1)


def swap_parts(vectors):
    width = LANES // CUTS
    part = lax.broadcasted_iota(jnp.int32, vectors[0].shape, 1) // width
    results = []
    for c in range(CUTS):
        result = vectors[c]
        for b in range(CUTS):
            if b != c:
                result = jnp.where(part == b, pltpu.roll(vectors[b], (b - c) % CUTS * width, 1), result)
        results.append(result)
    return results


def store_slices(ref, vectors):
    rows = ORDER // CUTS
    for a in range(rows):
        for c, vector in enumerate(swap_parts([vectors[a + rows * b] for b in range(CUTS)])):
            ref[pl.ds(rows * c + a, SUB, stride=ORDER), :] = vector


def load_slices(ref):
    rows = ORDER // CUTS
    vectors = [None] * ORDER
    for a in range(rows):
        parts = [ref[pl.ds(rows * c + a, SUB, stride=ORDER), :] for c in range(CUTS)]
        for b, vector in enumerate(swap_parts(parts)):
            vectors[a + rows * b] = vector
    return vectors


def pack_kernel(stream, taps, rates, residues, tail_ref, out_ref, taps_ref, rows_v, taps_v, rate_v, residue_v, sems):
    count, rows, chans = stream.shape
    held = rows_v.shape[1]
    offset = pl.multiple_of(lax.axis_index("dp") * chans, LANES)
    copies = [
        pltpu.make_async_copy(rates, rate_v, sems.at[0]),
        pltpu.make_async_copy(residues, residue_v, sems.at[1]),
        pltpu.make_async_copy(stream.at[:, pl.ds(rows - held, held), :], rows_v, sems.at[2]),
        pltpu.make_async_copy(taps.at[:, :, pl.ds(offset, chans)], taps_v, sems.at[3]),
    ]
    for copy in copies:
        copy.start()
    copies[0].wait()
    copies[1].wait()
    mask = low_half((rate_v.shape[0], LANES))
    for q in range(rate_v.shape[1] // LANES):
        rate = rate_v[:, q * LANES : (q + 1) * LANES]
        residue = residue_v[:, q * LANES : (q + 1) * LANES]
        out_ref[2 * q] = pick(mask, rate, half_turn(residue))
        out_ref[2 * q + 1] = pick(mask, half_turn(rate), residue)
    copies[2].wait()
    tail_ref[...] = rows_v[:, held - tail_ref.shape[1] :, :]
    copies[3].wait()
    blocks = chans // LANES
    for i in range(count):
        for lag in range(TAPS):
            for j in range(blocks):
                taps_ref[pl.ds((i * TAPS + lag) * blocks + j, 1), :] = taps_v[
                    i, pl.ds(lag, 1), j * LANES : (j + 1) * LANES
                ]


def features_kernel(stream_ref, halo_ref, taps_ref, product_ref, query_ref, wide_ref):
    rows = stream_ref.shape[1]
    blocks = stream_ref.shape[2] // LANES
    span = SUB * blocks
    for i in range(3):
        for j in range(blocks):
            cols = slice(j * LANES, (j + 1) * LANES)
            wide_ref[i, pl.ds(j * SUB + SUB - TAPS + 1, TAPS - 1), :] = halo_ref[i, :, cols].astype(F32)
            for pair in range(rows // (2 * SUB)):
                both = stream_ref[i, pair * 2 * SUB : (pair + 1) * 2 * SUB, cols].astype(F32)
                base = (2 * pair + 1) * span + j * SUB
                wide_ref[i, pl.ds(base, SUB), :] = both[:SUB]
                wide_ref[i, pl.ds(base + span, SUB), :] = both[SUB:]
    taps = [[taps_ref[pl.ds((i * TAPS + lag) * blocks, blocks), :] for lag in range(TAPS)] for i in range(3)]

    def token(i, start, s):
        return wide_ref[i, pl.ds(start + s, blocks, stride=SUB), :]

    def step(b, carry):
        before = [list(c) for c in carry]
        start = pl.multiple_of((b + 1) * span, span)
        for s in range(SUB):
            feats = []
            for i in range(3):
                now = token(i, start, s)
                older, old = before[i]
                feats.append(taps[i][0] * now + taps[i][1] * old + taps[i][2] * older)
                before[i] = [old, now]
            at = pl.multiple_of(b * span + s * blocks, blocks)
            query_ref[pl.ds(at, blocks), :] = feats[0]
            product_ref[pl.ds(at, blocks), :] = feats[1] * feats[2]
        return tuple(tuple(c) for c in before)

    first = tuple((token(i, 0, SUB - 2), token(i, 0, SUB - 1)) for i in range(3))
    lax.fori_loop(0, rows // SUB, step, first)


def state_kernel(product_ref, poles_ref, state_ref, decay_ref, residue_ref, rate_ref, wide_ref):
    blocks = SUB
    rows = product_ref.shape[0] // blocks
    poles = poles_ref[...]
    lane = lax.broadcasted_iota(jnp.int32, (ORDER, LANES), 1)
    for j in range(blocks):
        group = lane // GROUP + j * (LANES // GROUP)
        wide_ref[0, pl.ds(j * ORDER, ORDER), :] = jnp.take_along_axis(poles, group, axis=1)
        wide_ref[1, pl.ds(j * ORDER, ORDER), :] = jnp.take_along_axis(poles, group + LANES // 2, axis=1)
    rates, decays = [], []
    for r in range(ORDER):
        rate = wide_ref[0, pl.ds(r, blocks, stride=ORDER), :]
        decay = jnp.exp(-rate)
        decay_ref[pl.ds(r * blocks, blocks), :] = decay
        residue_ref[pl.ds(r * blocks, blocks), :] = wide_ref[1, pl.ds(r, blocks, stride=ORDER), :]
        rates.append(rate)
        decays.append(decay)
    store_slices(rate_ref, rates)

    def step(b, states):
        states = list(states)
        for s in range(SUB):
            p = product_ref[pl.ds(pl.multiple_of((b * SUB + s) * blocks, blocks), blocks), :]
            states = [decays[r] * states[r] + p for r in range(ORDER)]
        return tuple(states)

    zero = jnp.zeros((blocks, LANES), F32)
    store_slices(state_ref, lax.fori_loop(0, rows // SUB, step, (zero,) * ORDER))


def near_kernel(span, parts_ref, rate_ref, total_ref, decay_ref, far_ref, prefix_ref):
    count = parts_ref.shape[0]
    rate = rate_ref[lax.rem(lax.axis_index("ctx"), count)]
    decay = jnp.exp(-rate * float(span))
    decay_ref[...] = decay
    far_ref[...] = jnp.exp(-rate * float(span * count))
    run = jnp.zeros(rate.shape, F32)
    for k in range(count):
        prefix_ref[k] = run
        run = decay * run + parts_ref[k]
    total_ref[...] = run


def spread_kernel(run_ref, decay_ref, prefix_ref, out_ref):
    run = run_ref[...]
    for k in range(out_ref.shape[0]):
        out_ref[k] = prefix_ref[k] + run
        run = decay_ref[...] * run


def output_kernel(state_ref, product_ref, query_ref, decay_ref, residue_ref, out_ref, wide_ref):
    blocks = SUB
    span = SUB * blocks
    rows = product_ref.shape[0] // blocks
    decays = [decay_ref[pl.ds(r * blocks, blocks), :] for r in range(ORDER)]
    residues = [residue_ref[pl.ds(r * blocks, blocks), :] for r in range(ORDER)]

    def step(b, states):
        states = list(states)
        for s in range(SUB):
            at = pl.multiple_of((b * SUB + s) * blocks, blocks)
            p = product_ref[pl.ds(at, blocks), :]
            states = [decays[r] * states[r] + p for r in range(ORDER)]
            terms = [residues[r] * states[r] for r in range(ORDER)]
            while len(terms) > 1:
                terms = [terms[k] + terms[k + 1] for k in range(0, len(terms), 2)]
            wide_ref[pl.ds(b * span + s, blocks, stride=SUB), :] = query_ref[pl.ds(at, blocks), :] * terms[0]
        return tuple(states)

    lax.fori_loop(0, rows // SUB, step, tuple(load_slices(state_ref)))
    for pair in range(rows // (2 * SUB)):
        for j in range(blocks):
            base = 2 * pair * span + j * SUB
            both = jnp.concatenate([wide_ref[pl.ds(base, SUB), :], wide_ref[pl.ds(base + span, SUB), :]], 0)
            out_ref[pair * 2 * SUB : (pair + 1) * 2 * SUB, j * LANES : (j + 1) * LANES] = both.astype(jnp.bfloat16)


def shape(*dims):
    return pltpu.VMEM(dims, F32)


def call(kernel, out_shape, inputs, scratch=()):
    return pl.pallas_call(kernel, out_shape=out_shape, scratch_shapes=list(scratch))(
        *[pltpu.with_memory_space_constraint(x, pltpu.VMEM) for x in inputs]
    )


def exchange(x, groups):
    return lax.all_to_all(x, "ctx", split_axis=0, concat_axis=0, tiled=True, axis_index_groups=groups)


def earlier_runs(total, decay, run):
    def send(value, routes):
        pairs = [(a * run + k, b * run + k) for a, b in routes for k in range(run)]
        return lax.ppermute(value, "ctx", pairs)

    half = RUNS // 2
    before = None
    upto = total
    for z in range(half - 1):
        got = send(upto, [(z, z + 1)])
        before = got if before is None else before + got
        upto = decay * before + total
    got = {far: send(upto, [(z, z + far) for z in range(half - 1, RUNS - far)]) for far in JUMPS}
    later = got[half]
    for far in range(half - 1, 0, -1):
        later = decay * later + got[far]
    return before + later


def block(stream, short_taps, decay_rate, residue):
    rows, chans = stream.shape[1], stream.shape[2]
    blocks = chans // LANES
    ctx_size, dp_size = lax.axis_size("ctx"), lax.axis_size("dp")
    reach = TAPS - 1

    anywhere = pl.BlockSpec(memory_space=pl.ANY)
    tail, packed, taps = pl.pallas_call(
        pack_kernel,
        in_specs=[anywhere] * 4,
        out_shape=(
            pltpu.VMEM((3, reach, chans), stream.dtype),
            shape(dp_size, decay_rate.shape[0], LANES),
            shape(3 * TAPS * blocks, LANES),
        ),
        scratch_shapes=[
            pltpu.VMEM((3, 2 * SUB, chans), stream.dtype),
            pltpu.VMEM((3, TAPS, chans), F32),
            pltpu.VMEM(decay_rate.shape, F32),
            pltpu.VMEM(residue.shape, F32),
            pltpu.SemaphoreType.DMA((4,)),
        ],
        name="pack",
    )(stream, short_taps, decay_rate, residue)
    halo = lax.ppermute(tail, "ctx", [(k, k + 1) for k in range(ctx_size - 1)])
    poles = lax.all_to_all(packed, "dp", split_axis=0, concat_axis=0, tiled=True)
    poles = poles.reshape(ORDER, LANES)

    token_major = shape(rows * blocks, LANES)
    product, query = call(
        features_kernel,
        (token_major, token_major),
        (stream, halo, taps),
        (pltpu.VMEM((3, (rows // SUB + 1) * SUB * blocks, LANES), F32),),
    )
    table = shape(ORDER * blocks, LANES)
    state, decay, gain, rate = call(
        state_kernel, (table, table, table, table), (product, poles), (pltpu.VMEM((2, ORDER * blocks, LANES), F32),)
    )

    run = ctx_size // RUNS
    part = ORDER // CUTS
    near = [[z * run + k for k in range(run)] for z in range(RUNS)]
    parts = exchange(state.reshape(run, part, LANES), near)
    piece = shape(part, LANES)
    total, decay_near, decay_far, prefix = call(
        functools.partial(near_kernel, rows),
        (piece, piece, piece, shape(run, part, LANES)),
        (parts, rate.reshape(run, part, LANES)),
    )
    before = earlier_runs(total, decay_far, run)
    starts = call(spread_kernel, shape(run, part, LANES), (before, decay_near, prefix))
    start = exchange(starts, near)
    return call(
        output_kernel,
        jax.ShapeDtypeStruct((rows, chans), jnp.bfloat16),
        (start.reshape(ORDER * blocks, LANES), product, query, decay, gain),
        (pltpu.VMEM((rows * blocks, LANES), F32),),
    )


def solution(mesh):
    in_specs = (P(None, "ctx", "dp"), P(), P("dp", None), P("dp", None))
    out_specs = P("ctx", "dp")
    return jax.shard_map(block, mesh=mesh, in_specs=in_specs, out_specs=out_specs, check_vma=False)
```

time: 221 us -> 67 us (0.30)
  the two profiles are of different devices: /device:TPU:9 before, /device:TPU:907 now
where the time goes in v1:
time: 67 us; the launch traced here: 66.6 us
  blocking collectives  30.1 us (45%)
  starting transfers between devices  17.7 us (26%)
  waiting for transfers between devices  13.5 us (20%)
  Pallas kernels  5.18 us (8%)
    all_to_all x2, blocking collectives, exchange(): lax.all_to_all(x, 'ctx', split_axis=0, concat_axis=0, tiled=True, axis_in...  30.1 us
    ppermute x7, waiting for transfers between devices, send(): return lax.ppermute(value, 'ctx', pairs)  12.7 us
    ppermute x7, starting transfers between devices, send(): return lax.ppermute(value, 'ctx', pairs)  7.15 us
    ppermute x1, starting transfers between devices, block(): halo = lax.ppermute(tail, 'ctx', [(k, k + 1) for k in range(ctx_size - 1)])  5.33 us
    all_to_all x1, starting transfers between devices, block(): lax.all_to_all(packed, 'dp', split_axis=0, concat_axis=0, tiled=True)  5.18 us
    pallas_call x5, Pallas kernels, call(): pl.pallas_call(kernel, out_shape=out_shape, scratch_shapes=list(scratch))  3.53 us
    pallas_call x1, Pallas kernels, block(): pl.pallas_call(pack_kernel, in_specs=[anywhere] * 4, out_shape=(pltpu.VME...  1.64 us
  transfers between devices with their start and end apart: 9, of which 5 were waited for; matrix products, arithmetic and copies ran while one was open for 0% of the time, Pallas kernels for 1%

profile of v1, /device:TPU:907, one launch (start us, length us, event | category | flops | bytes accessed | tf_op | source)
XLA Modules:
  0.0 66.6 jit_solution(7344560475494817369)
XLA Ops:
  0.0 0.0 copy-start
  0.0 1.6 %pack.1 = (bf16[3,2,1024]{2,1,0:T(2,128)(2,1)S(1)}, f32[8,2,128]{2,1,0:T(2,128)}, f32[72,128]{1,0:T(8,128)S(1)}) custom-call(bf16[3,128,1024]{2,1,0:T(8,128)(2,1)} %stream_ref.1, f32[3,3,8192]{2,1,0:T(4,128)} %taps.1, f32[2,512]{1,0:T(2,128)} %rates.1, f32[2,512]{1,0:T(2,128)} %residues.1), custom_call_target="tpu_custom_call" | custom-call | tf_op jit(solution)/shard_map/pack/pallas_call | solution.py:250
  1.7 5.2 %all-to-all-start = ((f32[8,2,128]{2,1,0:T(2,128)}), f32[8,2,128]{2,1,0:T(2,128)S(1)}, u32[]{:S(2)}, u32[]{:S(2)}) async-start(f32[8,2,128]{2,1,0:T(2,128)} %get-tuple-element.21), calls=%async_computation | async-start | bytes 16384 | tf_op jit(solution)/shard_map/all_to_all | solution.py:268
  6.8 5.3 %collective-permute-start = (bf16[3,2,1024]{2,1,0:T(2,128)(2,1)S(1)}, bf16[3,2,1024]{2,1,0:T(2,128)(2,1)S(1)}, u32[]{:S(2)}, u32[]{:S(2)}) collective-permute-start(bf16[3,2,1024]{2,1,0:T(2,128)(2,1)S(1)} %get-tuple-element.18), channel_id=1, source_target_pairs={{0,8},{8,16},{16,24},{24,32},{32,40},{40,48},{48,56},{56,64},{64,7... | collective-permute-start | bytes 36872 | tf_op jit(solution)/shard_map/ppermute | solution.py:267
  12.2 0.8 %collective-permute-done.halo_ref = bf16[3,2,1024]{2,1,0:T(2,128)(2,1)S(1)} collective-permute-done((bf16[3,2,1024]{2,1,0:T(2,128)(2,1)S(1)}, bf16[3,2,1024]{2,1,0:T(2,128)(2,1)S(1)}, u32[]{:S(2)}, u32[]{:S(2)}) %collective-permute-start) | collective-permute-done | bytes 12320 | tf_op jit(solution)/shard_map/ppermute | solution.py:267
  13.0 0.0 copy-done
  13.0 0.6 shard_map.46
  13.6 0.0 all-to-all-done
  13.6 0.9 %shard_map.47 = (f32[128,128]{1,0:T(8,128)S(1)}, f32[128,128]{1,0:T(8,128)S(1)}, f32[128,128]{1,0:T(8,128)S(1)}, f32[128,128]{1,0:T(8,128)S(1)}) custom-call(f32[1024,128]{1,0:T(8,128)S(1)} %get-tuple-element.20.product_ref, f32[16,128]{1,0:T(8,128)S(1)} %bitcast.7), custom_call_target="tpu_custom_call" | custom-call | tf_op jit(solution)/shard_map/pallas_call | solution.py:215
  14.5 17.5 %all_to_all.15.parts_ref = f32[16,8,128]{2,1,0:T(8,128)S(1)} all-to-all(f32[16,8,128]{2,1,0:T(8,128)S(1)} %bitcast.6), channel_id=1, replica_groups={{0,8,16,24,32,40,48,56,64,72,80,88,96,104,112,120},{128,136,144,152,160..., dimensions={0} | all-to-all | bytes 131072 | tf_op jit(solution)/shard_map/all_to_all | solution.py:221
  32.0 0.7 collective-permute-start.1
  32.7 0.0 collective-permute-done.1
  32.7 0.7 collective-permute-start.2
  33.4 0.0 collective-permute-done.2
  33.4 0.7 collective-permute-start.3
  34.1 0.0 collective-permute-done.3
  34.1 1.3 %collective-permute-start.7 = (f32[8,128]{1,0:T(8,128)S(1)}, f32[8,128]{1,0:T(8,128)S(1)}, u32[]{:S(2)}, u32[]{:S(2)}) collective-permute-start(f32[8,128]{1,0:T(8,128)S(1)} %get-tuple-element.31), channel_id=1, source_target_pairs={{384,512},{392,520},{400,528},{408,536},{416,544},{424,552},{432,5... | collective-permute-start | bytes 12296 | tf_op jit(solution)/shard_map/ppermute | solution.py:227
  35.4 1.3 %collective-permute-start.6 = (f32[8,128]{1,0:T(8,128)S(1)}, f32[8,128]{1,0:T(8,128)S(1)}, u32[]{:S(2)}, u32[]{:S(2)}) collective-permute-start(f32[8,128]{1,0:T(8,128)S(1)} %get-tuple-element.31), channel_id=1, source_target_pairs={{384,640},{392,648},{400,656},{408,664},{416,672},{424,680},{432,6... | collective-permute-start | bytes 12296 | tf_op jit(solution)/shard_map/ppermute | solution.py:227
  36.7 1.3 %collective-permute-start.5 = (f32[8,128]{1,0:T(8,128)S(1)}, f32[8,128]{1,0:T(8,128)S(1)}, u32[]{:S(2)}, u32[]{:S(2)}) collective-permute-start(f32[8,128]{1,0:T(8,128)S(1)} %get-tuple-element.31), channel_id=1, source_target_pairs={{384,768},{392,776},{400,784},{408,792},{416,800},{424,808},{432,8... | collective-permute-start | bytes 12296 | tf_op jit(solution)/shard_map/ppermute | solution.py:227
  38.0 1.3 %collective-permute-start.4 = (f32[8,128]{1,0:T(8,128)S(1)}, f32[8,128]{1,0:T(8,128)S(1)}, u32[]{:S(2)}, u32[]{:S(2)}) collective-permute-start(f32[8,128]{1,0:T(8,128)S(1)} %get-tuple-element.31), channel_id=1, source_target_pairs={{384,896},{392,904},{400,912},{408,920},{416,928},{424,936},{432,9... | collective-permute-start | bytes 12296 | tf_op jit(solution)/shard_map/ppermute | solution.py:227
  39.3 0.1 collective-permute-done.7
  39.3 4.3 %collective-permute-done.6 = f32[8,128]{1,0:T(8,128)S(1)} collective-permute-done((f32[8,128]{1,0:T(8,128)S(1)}, f32[8,128]{1,0:T(8,128)S(1)}, u32[]{:S(2)}, u32[]{:S(2)}) %collective-permute-start.6) | collective-permute-done | bytes 4128 | tf_op jit(solution)/shard_map/ppermute | solution.py:227
  43.6 4.0 %collective-permute-done.5 = f32[8,128]{1,0:T(8,128)S(1)} collective-permute-done((f32[8,128]{1,0:T(8,128)S(1)}, f32[8,128]{1,0:T(8,128)S(1)}, u32[]{:S(2)}, u32[]{:S(2)}) %collective-permute-start.5) | collective-permute-done | bytes 4128 | tf_op jit(solution)/shard_map/ppermute | solution.py:227
  47.6 4.3 %collective-permute-done.4 = f32[8,128]{1,0:T(8,128)S(1)} collective-permute-done((f32[8,128]{1,0:T(8,128)S(1)}, f32[8,128]{1,0:T(8,128)S(1)}, u32[]{:S(2)}, u32[]{:S(2)}) %collective-permute-start.4) | collective-permute-done | bytes 4128 | tf_op jit(solution)/shard_map/ppermute | solution.py:227
  52.0 12.7 %all_to_all.16 = f32[16,8,128]{2,1,0:T(8,128)S(1)} all-to-all(f32[16,8,128]{2,1,0:T(8,128)S(1)} %shard_map.49), channel_id=1, replica_groups={{0,8,16,24,32,40,48,56,64,72,80,88,96,104,112,120},{128,136,144,152,160..., dimensions={0} | all-to-all | bytes 131072 | tf_op jit(solution)/shard_map/all_to_all | solution.py:221
  64.6 2.0 %shard_map.50 = bf16[128,1024]{1,0:T(8,128)(2,1)} custom-call(f32[128,128]{1,0:T(8,128)S(1)} %bitcast.4, f32[1024,128]{1,0:T(8,128)S(1)} %get-tuple-element.20.product_ref, f32[1024,128]{1,0:T(8,128)S(1)} %get-tuple-element.28.query_ref, f32[128,128]{1,0:T(8,128)S(1)} %get-tuple-element.29.decay_ref, f32[128,128]{1,0:T(8,128)S(1)} %get-tuple-element.30.residue_ref), custom_call_target="tpu_custom_call" | custom-call | tf_op jit(solution)/shard_map/pallas_call | solution.py:215
  (6 shorter events, 0.1 us)
Async XLA Ops:
  0.0 13.0 %copy-start = (bf16[3,128,1024]{2,1,0:T(8,128)(2,1)S(1)}, bf16[3,128,1024]{2,1,0:T(8,128)(2,1)}, u32[]{:S(2)}) copy-start(bf16[3,128,1024]{2,1,0:T(8,128)(2,1)} %stream_ref.1) | copy-start | bytes 2359300
  1.7 11.9 %all-to-all-start = ((f32[8,2,128]{2,1,0:T(2,128)}), f32[8,2,128]{2,1,0:T(2,128)S(1)}, u32[]{:S(2)}, u32[]{:S(2)}) async-start(f32[8,2,128]{2,1,0:T(2,128)} %get-tuple-element.21), calls=%async_computation | async-start | bytes 16384 | tf_op jit(solution)/shard_map/all_to_all | solution.py:268
  6.8 6.1 %collective-permute-start = (bf16[3,2,1024]{2,1,0:T(2,128)(2,1)S(1)}, bf16[3,2,1024]{2,1,0:T(2,128)(2,1)S(1)}, u32[]{:S(2)}, u32[]{:S(2)}) collective-permute-start(bf16[3,2,1024]{2,1,0:T(2,128)(2,1)S(1)} %get-tuple-element.18), channel_id=1, source_target_pairs={{0,8},{8,16},{16,24},{24,32},{32,40},{40,48},{48,56},{56,64},{64,7... | collective-permute-start | bytes 36872 | tf_op jit(solution)/shard_map/ppermute | solution.py:267
  32.0 0.7 %collective-permute-start.1 = (f32[8,128]{1,0:T(8,128)S(1)}, f32[8,128]{1,0:T(8,128)S(1)}, u32[]{:S(2)}, u32[]{:S(2)}) collective-permute-start(f32[8,128]{1,0:T(8,128)S(1)} %get-tuple-element.24), channel_id=1, source_target_pairs={{0,128},{8,136},{16,144},{24,152},{32,160},{40,168},{48,176},{56,1... | collective-permute-start | bytes 12296 | tf_op jit(solution)/shard_map/ppermute | solution.py:227
  32.7 0.7 %collective-permute-start.2 = (f32[8,128]{1,0:T(8,128)S(1)}, f32[8,128]{1,0:T(8,128)S(1)}, u32[]{:S(2)}, u32[]{:S(2)}) collective-permute-start(f32[8,128]{1,0:T(8,128)S(1)} %multiply_add_fusion.2), channel_id=1, source_target_pairs={{128,256},{136,264},{144,272},{152,280},{160,288},{168,296},{176,3... | collective-permute-start | bytes 12296 | tf_op jit(solution)/shard_map/ppermute | solution.py:227
  33.4 0.7 %collective-permute-start.3 = (f32[8,128]{1,0:T(8,128)S(1)}, f32[8,128]{1,0:T(8,128)S(1)}, u32[]{:S(2)}, u32[]{:S(2)}) collective-permute-start(f32[8,128]{1,0:T(8,128)S(1)} %get-tuple-element.33), channel_id=1, source_target_pairs={{256,384},{264,392},{272,400},{280,408},{288,416},{296,424},{304,4... | collective-permute-start | bytes 12296 | tf_op jit(solution)/shard_map/ppermute | solution.py:227
  34.1 5.3 %collective-permute-start.7 = (f32[8,128]{1,0:T(8,128)S(1)}, f32[8,128]{1,0:T(8,128)S(1)}, u32[]{:S(2)}, u32[]{:S(2)}) collective-permute-start(f32[8,128]{1,0:T(8,128)S(1)} %get-tuple-element.31), channel_id=1, source_target_pairs={{384,512},{392,520},{400,528},{408,536},{416,544},{424,552},{432,5... | collective-permute-start | bytes 12296 | tf_op jit(solution)/shard_map/ppermute | solution.py:227
  35.4 8.3 %collective-permute-start.6 = (f32[8,128]{1,0:T(8,128)S(1)}, f32[8,128]{1,0:T(8,128)S(1)}, u32[]{:S(2)}, u32[]{:S(2)}) collective-permute-start(f32[8,128]{1,0:T(8,128)S(1)} %get-tuple-element.31), channel_id=1, source_target_pairs={{384,640},{392,648},{400,656},{408,664},{416,672},{424,680},{432,6... | collective-permute-start | bytes 12296 | tf_op jit(solution)/shard_map/ppermute | solution.py:227
  36.7 11.0 %collective-permute-start.5 = (f32[8,128]{1,0:T(8,128)S(1)}, f32[8,128]{1,0:T(8,128)S(1)}, u32[]{:S(2)}, u32[]{:S(2)}) collective-permute-start(f32[8,128]{1,0:T(8,128)S(1)} %get-tuple-element.31), channel_id=1, source_target_pairs={{384,768},{392,776},{400,784},{408,792},{416,800},{424,808},{432,8... | collective-permute-start | bytes 12296 | tf_op jit(solution)/shard_map/ppermute | solution.py:227
  38.0 14.0 %collective-permute-start.4 = (f32[8,128]{1,0:T(8,128)S(1)}, f32[8,128]{1,0:T(8,128)S(1)}, u32[]{:S(2)}, u32[]{:S(2)}) collective-permute-start(f32[8,128]{1,0:T(8,128)S(1)} %get-tuple-element.31), channel_id=1, source_target_pairs={{384,896},{392,904},{400,912},{408,920},{416,928},{424,936},{432,9... | collective-permute-start | bytes 12296 | tf_op jit(solution)/shard_map/ppermute | solution.py:227

commit v2 on v1

v2 whole, which is shorter than its diff:
```python
import functools

import jax
import jax.numpy as jnp
from jax import lax
from jax.experimental import pallas as pl
from jax.experimental.pallas import tpu as pltpu
from jax.sharding import PartitionSpec as P


GROUP = 16
ORDER = 16
TAPS = 3
LANES = 128
SUB = 8
CUTS = 2
PART = ORDER // CUTS
EDGES = 5
SEND = PART + EDGES
BACK = PART + 3
RUNS = 8
CHAIN = 5
JUMPS = (3, 2, 1)
F32 = jnp.float32


def low_half(shape):
    return lax.broadcasted_iota(jnp.int32, shape, len(shape) - 1) < LANES // 2


def half_turn(x):
    return pltpu.roll(x, LANES // 2, x.ndim - 1)


def swap_halves(first, second):
    mask = low_half(first.shape)
    return jnp.where(mask, first, half_turn(second)), jnp.where(mask, half_turn(first), second)


def store_slices(ref, vectors, chunk):
    for a in range(PART):
        for c, vector in enumerate(swap_halves(vectors[a], vectors[a + PART])):
            ref[pl.ds(chunk * c + a, SUB, stride=CUTS * chunk), :] = vector


def load_pair(ref, row):
    return swap_halves(*[ref[pl.ds(BACK * c + row, SUB, stride=CUTS * BACK), :] for c in range(CUTS)])


def pack_kernel(stream, taps, rates, residues, out_ref, stream_ref, taps_ref, taps_v, rate_v, residue_v, sems):
    count, _, chans = taps_v.shape
    offset = pl.multiple_of(lax.axis_index("dp") * chans, LANES)
    copies = [
        pltpu.make_async_copy(rates, rate_v, sems.at[0]),
        pltpu.make_async_copy(residues, residue_v, sems.at[1]),
        pltpu.make_async_copy(taps.at[:, :, pl.ds(offset, chans)], taps_v, sems.at[2]),
        pltpu.make_async_copy(stream, stream_ref, sems.at[3]),
    ]
    for copy in copies:
        copy.start()
    copies[0].wait()
    copies[1].wait()
    mask = low_half((rate_v.shape[0], LANES))
    for q in range(rate_v.shape[1] // LANES):
        rate = rate_v[:, q * LANES : (q + 1) * LANES]
        residue = residue_v[:, q * LANES : (q + 1) * LANES]
        out_ref[2 * q] = jnp.where(mask, rate, half_turn(residue))
        out_ref[2 * q + 1] = jnp.where(mask, half_turn(rate), residue)
    copies[2].wait()
    blocks = chans // LANES
    for i in range(count):
        for lag in range(TAPS):
            for j in range(blocks):
                taps_ref[pl.ds((i * TAPS + lag) * blocks + j, 1), :] = taps_v[
                    i, pl.ds(lag, 1), j * LANES : (j + 1) * LANES
                ]
    copies[3].wait()


def spread_tokens(source_ref, wide_ref, pairs):
    blocks = source_ref.shape[1] // LANES
    span = SUB * blocks
    for pair in pairs:
        for j in range(blocks):
            both = source_ref[pair * 2 * SUB : (pair + 1) * 2 * SUB, j * LANES : (j + 1) * LANES].astype(F32)
            base = 2 * pair * span + j * SUB
            wide_ref[pl.ds(base, SUB), :] = both[:SUB]
            wide_ref[pl.ds(base + span, SUB), :] = both[SUB:]


def load_taps(taps_ref, blocks, i):
    return [taps_ref[pl.ds((i * TAPS + lag) * blocks, blocks), :] for lag in range(TAPS)]


def features_kernel(stream_ref, taps_ref, after_ref, product_ref, edge_ref, wide_ref):
    rows = stream_ref.shape[1]
    blocks = stream_ref.shape[2] // LANES
    span = SUB * blocks
    last_pair = rows // (2 * SUB) - 1
    for i in range(3):
        spread_tokens(stream_ref.at[i], wide_ref.at[i], range(last_pair + 1) if i else (last_pair,))
    taps = [load_taps(taps_ref, blocks, i) for i in range(3)]

    def token(i, start, s):
        return wide_ref[i, pl.ds(start + s, blocks, stride=SUB), :]

    def step(b, carry):
        before = [list(c) for c in carry]
        start = pl.multiple_of(b * span, span)
        for s in range(SUB):
            feats = []
            for i in (1, 2):
                now = token(i, start, s)
                older, old = before[i - 1]
                feats.append(taps[i][0] * now + taps[i][1] * old + taps[i][2] * older)
                before[i - 1] = [old, now]
            product_ref[pl.ds(pl.multiple_of(b * span + s * blocks, blocks), blocks), :] = feats[0] * feats[1]
        return tuple(tuple(c) for c in before)

    zero = jnp.zeros((blocks, LANES), F32)
    lax.fori_loop(0, rows // SUB, step, ((zero, zero),) * 2)

    def put(row, value):
        edge_ref[pl.ds(row * blocks, blocks), :] = value

    for i in range(3):
        old, now = token(i, (rows - SUB) * blocks, SUB - 2), token(i, (rows - SUB) * blocks, SUB - 1)
        put(2 * i, taps[i][1] * now + taps[i][2] * old)
        put(2 * i + 1, taps[i][2] * now)
    for i in (1, 2):
        first, second = token(i, 0, 0), token(i, 0, 1)
        put(2 * i + 4, taps[i][0] * first)
        put(2 * i + 5, taps[i][0] * second + taps[i][1] * first)
    product_ref[pl.ds(0, blocks), :] = zero
    product_ref[pl.ds(blocks, blocks), :] = zero


def state_kernel(product_ref, poles_ref, edge_ref, state_ref, decay_ref, residue_ref, rate_ref, wide_ref):
    blocks = SUB
    rows = product_ref.shape[0] // blocks
    poles = poles_ref[...]
    lane = lax.broadcasted_iota(jnp.int32, (ORDER, LANES), 1)
    for j in range(blocks):
        group = lane // GROUP + j * (LANES // GROUP)
        wide_ref[0, pl.ds(j * ORDER, ORDER), :] = jnp.take_along_axis(poles, group, axis=1)
        wide_ref[1, pl.ds(j * ORDER, ORDER), :] = jnp.take_along_axis(poles, group + LANES // 2, axis=1)
    rates, decays = [], []
    for r in range(ORDER):
        rate = wide_ref[0, pl.ds(r, blocks, stride=ORDER), :]
        decay = jnp.exp(-rate)
        decay_ref[pl.ds(r * blocks, blocks), :] = decay
        residue_ref[pl.ds(r * blocks, blocks), :] = wide_ref[1, pl.ds(r, blocks, stride=ORDER), :]
        rates.append(rate)
        decays.append(decay)
    store_slices(rate_ref, rates, PART)
    for n in range(EDGES):
        parts = swap_halves(*[edge_ref[pl.ds((2 * n + t) * blocks, blocks), :] for t in range(2)])
        for c in range(CUTS):
            state_ref[pl.ds(SEND * c + PART + n, SUB, stride=CUTS * SEND), :] = parts[c]
    zero = jnp.zeros((blocks, LANES), F32)

    def step(b, states):
        states = list(states)
        for s in range(SUB):
            p = product_ref[pl.ds(pl.multiple_of((b * SUB + s) * blocks, blocks), blocks), :]
            states = [decays[r] * states[r] + p for r in range(ORDER)]
        return tuple(states)

    store_slices(state_ref, lax.fori_loop(0, rows // SUB, step, (zero,) * ORDER), SEND)


def local_kernel(product_ref, decay_ref, residue_ref, taps_ref, after_ref, stream, out_ref, query_ref, source_v, wide_ref, sem):
    blocks = SUB
    span = SUB * blocks
    rows = product_ref.shape[0] // blocks
    copy = pltpu.make_async_copy(stream.at[0], source_v, sem.at[0])
    copy.start()
    decays = [decay_ref[pl.ds(r * blocks, blocks), :] for r in range(ORDER)]
    residues = [residue_ref[pl.ds(r * blocks, blocks), :] for r in range(ORDER)]

    def step(b, states):
        states = list(states)
        for s in range(SUB):
            at = pl.ds(pl.multiple_of((b * SUB + s) * blocks, blocks), blocks)
            p = product_ref[at, :]
            states = [decays[r] * states[r] + p for r in range(ORDER)]
            out_ref[at, :] = total([residues[r] * states[r] for r in range(ORDER)])
        return tuple(states)

    zero = jnp.zeros((blocks, LANES), F32)
    lax.fori_loop(0, rows // SUB, step, (zero,) * ORDER)
    copy.wait()
    spread_tokens(source_v, wide_ref, range(rows // (2 * SUB)))
    taps = load_taps(taps_ref, blocks, 0)

    def filtered(b, before):
        older, old = before
        for s in range(SUB):
            now = wide_ref[pl.ds(pl.multiple_of(b * span, span) + s, blocks, stride=SUB), :]
            at = pl.ds(pl.multiple_of((b * SUB + s) * blocks, blocks), blocks)
            query_ref[at, :] = taps[0] * now + taps[1] * old + taps[2] * older
            older, old = old, now
        return older, old

    lax.fori_loop(0, rows // SUB, filtered, (zero, zero))


def total(terms):
    while len(terms) > 1:
        terms = [terms[k] + terms[k + 1] for k in range(0, len(terms), 2)]
    return terms[0]


def edge_state(own, previous, powers_ref):
    product = (own[3:4] + previous[1:2]) * (own[4:5] + previous[2:3])
    mask = low_half(product.shape)
    turned = half_turn(product)
    return powers_ref[0] * jnp.where(mask, product, turned) + powers_ref[1] * jnp.where(mask, turned, product)


def near_kernel(rows, parts_ref, rate_ref, message_ref, powers_ref, prefix_ref, halo_ref):
    count = parts_ref.shape[0] // SEND
    position = lax.axis_index("ctx")
    rate = rate_ref[lax.rem(position, count)]
    for n, length in enumerate((rows - 1, rows - 2, rows, rows * (count - 1), rows * count)):
        powers_ref[n] = jnp.exp(-rate * float(length))
    run = jnp.zeros(rate.shape, F32)
    none = jnp.zeros((3, LANES), F32)
    previous = none
    halo_ref[:3, :] = none
    for k in range(count):
        prefix_ref[k] = run
        new = parts_ref[pl.ds(SEND * k, PART), :]
        edges = parts_ref[pl.ds(SEND * k + PART, EDGES), :]
        if k:
            halo_ref[pl.ds(3 * k, 3), :] = previous
            new = new + edge_state(edges, previous, powers_ref)
        run = powers_ref[2] * run + new
        previous = edges[:3]
    first = parts_ref[pl.ds(PART, EDGES), :]
    start = run + powers_ref[3] * edge_state(first, none, powers_ref)
    message_ref[:PART, :] = jnp.where(position < count, start, run)
    message_ref[pl.ds(PART, 3), :] = previous
    message_ref[pl.ds(PART + 3, 2), :] = first[3:]


def link_kernel(z, count, message_ref, heard_ref, got_ref, powers_ref, message_out, heard_out):
    heard_out[...] = heard_ref[...] + got_ref[...]
    mine = message_ref[:PART, :]
    edges = message_ref[pl.ds(PART, EDGES), :]
    whole = powers_ref[4] * got_ref[:PART, :] + mine
    whole = whole + powers_ref[3] * edge_state(edges, got_ref[pl.ds(PART, EDGES), :], powers_ref)
    message_out[:PART, :] = jnp.where(lax.axis_index("ctx") // count == z + 1, whole, mine)
    message_out[pl.ds(PART, EDGES), :] = edges


def spread_kernel(message_ref, heard_ref, jumps_ref, powers_ref, prefix_ref, halo_ref, out_ref):
    count = prefix_ref.shape[0]
    index = lax.axis_index("ctx") // count
    run = heard_ref[:PART, :]
    halo = heard_ref[pl.ds(PART, EDGES), :]
    for n, far in enumerate(JUMPS):
        source = index - far
        value = jumps_ref[n][:PART, :]
        edges = jumps_ref[n][pl.ds(PART, EDGES), :]
        later = powers_ref[4] * run + value + powers_ref[3] * edge_state(edges, halo, powers_ref)
        run = jnp.where(source == CHAIN - 1, value, jnp.where(source >= CHAIN, later, run))
        halo = jnp.where(source >= CHAIN - 1, edges, halo)
    first = edge_state(message_ref[pl.ds(PART, EDGES), :], halo, powers_ref)
    for k in range(count):
        out_ref[pl.ds(BACK * k, PART), :] = prefix_ref[k] + run
        out_ref[pl.ds(BACK * k + PART, 3), :] = halo_ref[pl.ds(3 * k, 3), :] if k else halo[:3]
        run = powers_ref[2] * run
        if k == 0:
            run = run + first


def output_kernel(start_ref, product_ref, query_ref, edge_ref, local_ref, decay_ref, residue_ref, out_ref, wide_ref):
    blocks = SUB
    span = SUB * blocks
    rows = product_ref.shape[0] // blocks
    decays = [decay_ref[pl.ds(r * blocks, blocks), :] for r in range(ORDER)]
    residues = [residue_ref[pl.ds(r * blocks, blocks), :] for r in range(ORDER)]
    pairs = [load_pair(start_ref, a) for a in range(PART)]
    states = [low for low, _ in pairs] + [high for _, high in pairs]

    halos = [load_pair(start_ref, PART + n) for n in range(3)]
    carried = states
    for s in range(TAPS - 1):
        one, two = [edge_ref[pl.ds((2 * n + s) * blocks, blocks), :] + halos[n - 2][s] for n in (3, 4)]
        carried = [decays[r] * carried[r] + one * two for r in range(ORDER)]
        terms = [residues[r] * carried[r] for r in range(ORDER)]
        q = query_ref[pl.ds(s * blocks, blocks), :] + halos[0][s]
        wide_ref[pl.ds(s, blocks, stride=SUB), :] = q * total(terms)

    def token(b, s, terms):
        at = pl.ds(pl.multiple_of((b * SUB + s) * blocks, blocks), blocks)
        terms = [decays[r] * terms[r] for r in range(ORDER)]
        wide_ref[pl.ds(b * span + s, blocks, stride=SUB), :] = query_ref[at, :] * (local_ref[at, :] + total(terms))
        return terms

    def step(b, terms):
        terms = list(terms)
        for s in range(SUB):
            terms = token(b, s, terms)
        return tuple(terms)

    for s in range(TAPS - 1, SUB):
        terms = token(0, s, terms)
    lax.fori_loop(1, rows // SUB, step, tuple(terms))
    for pair in range(rows // (2 * SUB)):
        for j in range(blocks):
            base = 2 * pair * span + j * SUB
            both = jnp.concatenate([wide_ref[pl.ds(base, SUB), :], wide_ref[pl.ds(base + span, SUB), :]], 0)
            out_ref[pair * 2 * SUB : (pair + 1) * 2 * SUB, j * LANES : (j + 1) * LANES] = both.astype(jnp.bfloat16)


def shape(*dims):
    return pltpu.VMEM(dims, F32)


def call(kernel, out_shape, inputs, scratch=()):
    return pl.pallas_call(kernel, out_shape=out_shape, scratch_shapes=list(scratch))(
        *[pltpu.with_memory_space_constraint(x, pltpu.VMEM) for x in inputs]
    )


def exchange(x, groups):
    flat = x.reshape(len(groups[0]), 1, -1)
    flat = lax.all_to_all(flat, "ctx", split_axis=0, concat_axis=0, tiled=True, axis_index_groups=groups)
    return flat.reshape(x.shape)


def earlier_runs(message, powers, run):
    def send(value, routes):
        pairs = [(a * run + k, b * run + k) for a, b in routes for k in range(run)]
        return lax.ppermute(value, "ctx", pairs)

    heard = jnp.zeros((SEND, LANES), F32)
    row = shape(SEND, LANES)
    for z in range(CHAIN - 1):
        got = send(message, [(z, z + 1)])
        message, heard = call(functools.partial(link_kernel, z, run), (row, row), (message, heard, got, powers))
    jumps = [send(message, [(z, z + far) for z in range(CHAIN - 1, RUNS - far)]) for far in JUMPS]
    return message, heard, jumps


def block(stream, short_taps, decay_rate, residue):
    rows, chans = stream.shape[1], stream.shape[2]
    blocks = chans // LANES
    ctx_size, dp_size = lax.axis_size("ctx"), lax.axis_size("dp")

    packed, near_stream, taps = pl.pallas_call(
        pack_kernel,
        in_specs=[pl.BlockSpec(memory_space=pl.ANY)] * 4,
        out_shape=(
            shape(dp_size, decay_rate.shape[0], LANES),
            pltpu.VMEM(stream.shape, stream.dtype),
            shape(3 * TAPS * blocks, LANES),
        ),
        scratch_shapes=[
            pltpu.VMEM((3, TAPS, chans), F32),
            pltpu.VMEM(decay_rate.shape, F32),
            pltpu.VMEM(residue.shape, F32),
            pltpu.SemaphoreType.DMA((4,)),
        ],
        name="pack",
    )(stream, short_taps, decay_rate, residue)
    poles = lax.all_to_all(packed, "dp", split_axis=0, concat_axis=0, tiled=True)
    poles = poles.reshape(ORDER, LANES)

    token_major = shape(rows * blocks, LANES)
    product, edges = call(
        features_kernel,
        (token_major, shape(2 * EDGES * blocks, LANES)),
        (near_stream, taps, poles),
        (pltpu.VMEM((3, rows * blocks, LANES), F32),),
    )
    table = shape(ORDER * blocks, LANES)
    run = ctx_size // RUNS
    state, decay, gain, rate = call(
        state_kernel,
        (shape(run * SEND, LANES), table, table, table),
        (product, poles, edges),
        (pltpu.VMEM((2, ORDER * blocks, LANES), F32),),
    )

    near = [[z * run + k for k in range(run)] for z in range(RUNS)]
    parts = exchange(state, near)
    message, powers, prefix, halos = call(
        functools.partial(near_kernel, rows),
        (shape(SEND, LANES), shape(5, PART, LANES), shape(run, PART, LANES), shape(3 * run, LANES)),
        (parts, rate.reshape(run, PART, LANES)),
    )
    vmem = functools.partial(pltpu.with_memory_space_constraint, memory_space=pltpu.VMEM)
    local, query = pl.pallas_call(
        local_kernel,
        in_specs=[pl.BlockSpec(memory_space=pltpu.VMEM)] * 5 + [pl.BlockSpec(memory_space=pl.ANY)],
        out_shape=(token_major, token_major),
        scratch_shapes=[
            pltpu.VMEM((rows, chans), stream.dtype),
            pltpu.VMEM((rows * blocks, LANES), F32),
            pltpu.SemaphoreType.DMA((1,)),
        ],
        name="local",
    )(vmem(product), vmem(decay), vmem(gain), vmem(taps), vmem(message), stream)
    message, heard, jumps = earlier_runs(message, powers, run)

    def spread(message_ref, heard_ref, *refs):
        spread_kernel(message_ref, heard_ref, refs[: len(jumps)], *refs[len(jumps) :])

    starts = call(spread, shape(run * BACK, LANES), (message, heard, *jumps, powers, prefix, halos))
    return call(
        output_kernel,
        jax.ShapeDtypeStruct((rows, chans), jnp.bfloat16),
        (exchange(starts, near), product, query, edges, local, decay, gain),
        (pltpu.VMEM((rows * blocks, LANES), F32),),
    )


def solution(mesh):
    in_specs = (P(None, "ctx", "dp"), P(), P("dp", None), P("dp", None))
    out_specs = P("ctx", "dp")
    return jax.shard_map(block, mesh=mesh, in_specs=in_specs, out_specs=out_specs, check_vma=False)
```

time: 67 us -> 64.6 us (0.964)
  the two profiles are of different devices: /device:TPU:907 before, /device:TPU:897 now
where the time goes in v2:
time: 64.6 us; the launch traced here: 64.2 us
  blocking collectives  27.2 us (42%)
  waiting for transfers between devices  16.7 us (26%)
  starting transfers between devices  13.6 us (21%)
  Pallas kernels  6.57 us (10%)
    all_to_all x1, blocking collectives, exchange(): lax.all_to_all(flat, 'ctx', split_axis=0, concat_axis=0, tiled=True, axis...  17.3 us
    all_to_all x1, blocking collectives, block(): lax.all_to_all(packed, 'dp', split_axis=0, concat_axis=0, tiled=True)  9.87 us
    ppermute x7, waiting for transfers between devices, send(): return lax.ppermute(value, 'ctx', pairs)  9.71 us
    all_to_all x1, starting transfers between devices, exchange(): lax.all_to_all(flat, 'ctx', split_axis=0, concat_axis=0, tiled=True, axis...  7.16 us
    all_to_all x1, waiting for transfers between devices, exchange(): lax.all_to_all(flat, 'ctx', split_axis=0, concat_axis=0, tiled=True, axis...  6.95 us
    ppermute x7, starting transfers between devices, send(): return lax.ppermute(value, 'ctx', pairs)  6.48 us
    pallas_call x9, Pallas kernels, call(): pl.pallas_call(kernel, out_shape=out_shape, scratch_shapes=list(scratch))  3.98 us
    pallas_call x1, Pallas kernels, block(): pl.pallas_call(local_kernel, in_specs=[pl.BlockSpec(memory_space=pltpu.VM...  1.37 us
  transfers between devices with their start and end apart: 8, of which 4 were waited for; matrix products, arithmetic and copies ran while one was open for 0% of the time, Pallas kernels for 2%

profile of v2, /device:TPU:897, one launch (start us, length us, event | category | flops | bytes accessed | tf_op | source)
XLA Modules:
  0.0 64.2 jit_solution(10435158058048055301)
XLA Ops:
  0.0 1.2 %pack.1 = (f32[8,2,128]{2,1,0:T(2,128)S(1)}, bf16[3,128,1024]{2,1,0:T(8,128)(2,1)S(1)}, f32[72,128]{1,0:T(8,128)S(1)}) custom-call(bf16[3,128,1024]{2,1,0:T(8,128)(2,1)} %stream.3, f32[3,3,8192]{2,1,0:T(4,128)} %taps.1, f32[2,512]{1,0:T(2,128)} %rates.1, f32[2,512]{1,0:T(2,128)} %residues.1), custom_call_target="tpu_custom_call" | custom-call | tf_op jit(solution)/shard_map/pack/pallas_call | solution.py:353
  1.2 9.9 %all_to_all.15 = f32[8,2,128]{2,1,0:T(2,128)S(1)} all-to-all(f32[8,2,128]{2,1,0:T(2,128)S(1)} %get-tuple-element.30), channel_id=1, replica_groups=mesh['ctx'=128,'dp'=8] {'dp'}, dimensions={0} | all-to-all | bytes 16384 | tf_op jit(solution)/shard_map/all_to_all | solution.py:369
  11.1 0.4 shard_map.46
  11.5 0.9 %shard_map.47 = (f32[208,128]{1,0:T(8,128)S(1)}, f32[128,128]{1,0:T(8,128)S(1)}, f32[128,128]{1,0:T(8,128)S(1)}, f32[128,128]{1,0:T(8,128)S(1)}) custom-call(f32[1024,128]{1,0:T(8,128)S(1)} %get-tuple-element.31.product_ref, f32[16,128]{1,0:T(8,128)S(1)} %bitcast.10, f32[80,128]{1,0:T(8,128)S(1)} %get-tuple-element.32.edge_ref), custom_call_target="tpu_custom_call" | custom-call | tf_op jit(solution)/shard_map/pallas_call | solution.py:323
  12.4 17.3 %all_to_all.16 = f32[16,1,1664]{2,1,0:T(1,128)S(1)} all-to-all(f32[16,1,1664]{2,1,0:T(1,128)S(1)} %bitcast.8), channel_id=1, replica_groups={{0,8,16,24,32,40,48,56,64,72,80,88,96,104,112,120},{128,136,144,152,160..., dimensions={0} | all-to-all | bytes 212992 | tf_op jit(solution)/shard_map/all_to_all | solution.py:330
  29.8 0.1 shard_map.48
  29.9 0.7 %collective-permute-start = (f32[13,128]{1,0:T(8,128)S(1)}, f32[13,128]{1,0:T(8,128)S(1)}, u32[]{:S(2)}, u32[]{:S(2)}) collective-permute-start(f32[13,128]{1,0:T(8,128)S(1)} %get-tuple-element.35.message_ref.after_ref), channel_id=1, source_target_pairs={{0,128},{8,136},{16,144},{24,152},{32,160},{40,168},{48,176},{56,1... | collective-permute-start | bytes 19976 | tf_op jit(solution)/shard_map/ppermute | solution.py:337
  30.5 0.0 collective-permute-done.got_ref
  30.6 0.1 shard_map.49
  30.6 0.7 %collective-permute-start.1 = (f32[13,128]{1,0:T(8,128)S(1)}, f32[13,128]{1,0:T(8,128)S(1)}, u32[]{:S(2)}, u32[]{:S(2)}) collective-permute-start(f32[13,128]{1,0:T(8,128)S(1)} %get-tuple-element.37.message_ref), channel_id=1, source_target_pairs={{128,256},{136,264},{144,272},{152,280},{160,288},{168,296},{176,3... | collective-permute-start | bytes 19976 | tf_op jit(solution)/shard_map/ppermute | solution.py:337
  31.3 0.0 collective-permute-done.1.got_ref
  31.3 0.1 shard_map.50
  31.4 0.7 %collective-permute-start.2 = (f32[13,128]{1,0:T(8,128)S(1)}, f32[13,128]{1,0:T(8,128)S(1)}, u32[]{:S(2)}, u32[]{:S(2)}) collective-permute-start(f32[13,128]{1,0:T(8,128)S(1)} %get-tuple-element.39.message_ref), channel_id=1, source_target_pairs={{256,384},{264,392},{272,400},{280,408},{288,416},{296,424},{304,4... | collective-permute-start | bytes 19976 | tf_op jit(solution)/shard_map/ppermute | solution.py:337
  32.0 0.0 collective-permute-done.2.got_ref
  32.1 0.1 shard_map.51
  32.1 0.7 %collective-permute-start.3 = (f32[13,128]{1,0:T(8,128)S(1)}, f32[13,128]{1,0:T(8,128)S(1)}, u32[]{:S(2)}, u32[]{:S(2)}) collective-permute-start(f32[13,128]{1,0:T(8,128)S(1)} %get-tuple-element.41.message_ref), channel_id=1, source_target_pairs={{384,512},{392,520},{400,528},{408,536},{416,544},{424,552},{432,5... | collective-permute-start | bytes 19976 | tf_op jit(solution)/shard_map/ppermute | solution.py:337
  32.8 0.0 collective-permute-done.3.got_ref
  32.8 0.1 shard_map.52
  32.9 1.3 %collective-permute-start.6 = (f32[13,128]{1,0:T(8,128)S(1)}, f32[13,128]{1,0:T(8,128)S(1)}, u32[]{:S(2)}, u32[]{:S(2)}) collective-permute-start(f32[13,128]{1,0:T(8,128)S(1)} %get-tuple-element.43.message_ref), channel_id=1, source_target_pairs={{512,640},{520,648},{528,656},{536,664},{544,672},{552,680},{560,6... | collective-permute-start | bytes 19976 | tf_op jit(solution)/shard_map/ppermute | solution.py:337
  34.2 1.3 %collective-permute-start.5 = (f32[13,128]{1,0:T(8,128)S(1)}, f32[13,128]{1,0:T(8,128)S(1)}, u32[]{:S(2)}, u32[]{:S(2)}) collective-permute-start(f32[13,128]{1,0:T(8,128)S(1)} %get-tuple-element.43.message_ref), channel_id=1, source_target_pairs={{512,768},{520,776},{528,784},{536,792},{544,800},{552,808},{560,8... | collective-permute-start | bytes 19976 | tf_op jit(solution)/shard_map/ppermute | solution.py:337
  35.5 1.3 %collective-permute-start.4 = (f32[13,128]{1,0:T(8,128)S(1)}, f32[13,128]{1,0:T(8,128)S(1)}, u32[]{:S(2)}, u32[]{:S(2)}) collective-permute-start(f32[13,128]{1,0:T(8,128)S(1)} %get-tuple-element.43.message_ref), channel_id=1, source_target_pairs={{512,896},{520,904},{528,912},{536,920},{544,928},{552,936},{560,9... | collective-permute-start | bytes 19976 | tf_op jit(solution)/shard_map/ppermute | solution.py:337
  36.8 1.4 %collective-permute-done.6.refs_2_ = f32[13,128]{1,0:T(8,128)S(1)} collective-permute-done((f32[13,128]{1,0:T(8,128)S(1)}, f32[13,128]{1,0:T(8,128)S(1)}, u32[]{:S(2)}, u32[]{:S(2)}) %collective-permute-start.6) | collective-permute-done | bytes 6688 | tf_op jit(solution)/shard_map/ppermute | solution.py:337
  38.2 4.3 %collective-permute-done.5.refs_1_ = f32[13,128]{1,0:T(8,128)S(1)} collective-permute-done((f32[13,128]{1,0:T(8,128)S(1)}, f32[13,128]{1,0:T(8,128)S(1)}, u32[]{:S(2)}, u32[]{:S(2)}) %collective-permute-start.5) | collective-permute-done | bytes 6688 | tf_op jit(solution)/shard_map/ppermute | solution.py:337
  42.5 4.0 %collective-permute-done.4.refs_0_ = f32[13,128]{1,0:T(8,128)S(1)} collective-permute-done((f32[13,128]{1,0:T(8,128)S(1)}, f32[13,128]{1,0:T(8,128)S(1)}, u32[]{:S(2)}, u32[]{:S(2)}) %collective-permute-start.4) | collective-permute-done | bytes 6688 | tf_op jit(solution)/shard_map/ppermute | solution.py:337
  46.5 0.8 %shard_map.53 = f32[176,128]{1,0:T(8,128)} custom-call(f32[13,128]{1,0:T(8,128)S(1)} %get-tuple-element.43.message_ref, f32[13,128]{1,0:T(8,128)S(1)} %get-tuple-element.44.heard_ref, f32[13,128]{1,0:T(8,128)S(1)} %collective-permute-done.4.refs_0_, f32[13,128]{1,0:T(8,128)S(1)} %collective-permute-done.5.refs_1_, ...), custom_call_target="tpu_custom_call" | custom-call | tf_op jit(solution)/shard_map/pallas_call | solution.py:323
  47.2 7.2 %all-to-all-start.2 = ((f32[16,1,1408]{2,1,0:T(1,128)}), f32[16,1,1408]{2,1,0:T(1,128)S(1)}, u32[]{:S(2)}, u32[]{:S(2)}) async-start(f32[16,1,1408]{2,1,0:T(1,128)} %bitcast.4), calls=%async_computation.2 | async-start | bytes 180224 | tf_op jit(solution)/shard_map/all_to_all | solution.py:330
  54.4 1.4 %local.1 = (f32[1024,128]{1,0:T(8,128)S(1)}, f32[1024,128]{1,0:T(8,128)S(1)}) custom-call(f32[1024,128]{1,0:T(8,128)S(1)} %get-tuple-element.31.product_ref, f32[128,128]{1,0:T(8,128)S(1)} %get-tuple-element.47.decay_ref, f32[128,128]{1,0:T(8,128)S(1)} %get-tuple-element.48.residue_ref, f32[72,128]{1,0:T(8,128)S(1)} %get-tuple-element.29.taps_ref, ...), custom_call_target="tpu_custom_call" | custom-call | tf_op jit(solution)/shard_map/local/pallas_call | solution.py:396
  55.8 6.9 %all-to-all-done.2 = f32[16,1,1408]{2,1,0:T(1,128)S(1)} async-done(((f32[16,1,1408]{2,1,0:T(1,128)}), f32[16,1,1408]{2,1,0:T(1,128)S(1)}, u32[]{:S(2)}, u32[]{:S(2)}) %all-to-all-start.2) | async-done | bytes 90144 | tf_op jit(solution)/shard_map/all_to_all | solution.py:330
  62.7 1.5 %shard_map.54 = bf16[128,1024]{1,0:T(8,128)(2,1)} custom-call(f32[176,128]{1,0:T(8,128)S(1)} %bitcast.7, f32[1024,128]{1,0:T(8,128)S(1)} %get-tuple-element.31.product_ref, f32[1024,128]{1,0:T(8,128)S(1)} %get-tuple-element.49.query_ref, f32[80,128]{1,0:T(8,128)S(1)} %get-tuple-element.32.edge_ref, f32[1024,128]{1,0:T(8,128)S(1)} %get-tuple-element.50.local_ref, ...), custom_call_target="tpu_custom_call" | custom-call | tf_op jit(solution)/shard_map/pallas_call | solution.py:323
  (1 shorter events, 0.0 us)
Async XLA Ops:
  29.9 0.7 %collective-permute-start = (f32[13,128]{1,0:T(8,128)S(1)}, f32[13,128]{1,0:T(8,128)S(1)}, u32[]{:S(2)}, u32[]{:S(2)}) collective-permute-start(f32[13,128]{1,0:T(8,128)S(1)} %get-tuple-element.35.message_ref.after_ref), channel_id=1, source_target_pairs={{0,128},{8,136},{16,144},{24,152},{32,160},{40,168},{48,176},{56,1... | collective-permute-start | bytes 19976 | tf_op jit(solution)/shard_map/ppermute | solution.py:337
  30.6 0.7 %collective-permute-start.1 = (f32[13,128]{1,0:T(8,128)S(1)}, f32[13,128]{1,0:T(8,128)S(1)}, u32[]{:S(2)}, u32[]{:S(2)}) collective-permute-start(f32[13,128]{1,0:T(8,128)S(1)} %get-tuple-element.37.message_ref), channel_id=1, source_target_pairs={{128,256},{136,264},{144,272},{152,280},{160,288},{168,296},{176,3... | collective-permute-start | bytes 19976 | tf_op jit(solution)/shard_map/ppermute | solution.py:337
  31.4 0.7 %collective-permute-start.2 = (f32[13,128]{1,0:T(8,128)S(1)}, f32[13,128]{1,0:T(8,128)S(1)}, u32[]{:S(2)}, u32[]{:S(2)}) collective-permute-start(f32[13,128]{1,0:T(8,128)S(1)} %get-tuple-element.39.message_ref), channel_id=1, source_target_pairs={{256,384},{264,392},{272,400},{280,408},{288,416},{296,424},{304,4... | collective-permute-start | bytes 19976 | tf_op jit(solution)/shard_map/ppermute | solution.py:337
  32.1 0.7 %collective-permute-start.3 = (f32[13,128]{1,0:T(8,128)S(1)}, f32[13,128]{1,0:T(8,128)S(1)}, u32[]{:S(2)}, u32[]{:S(2)}) collective-permute-start(f32[13,128]{1,0:T(8,128)S(1)} %get-tuple-element.41.message_ref), channel_id=1, source_target_pairs={{384,512},{392,520},{400,528},{408,536},{416,544},{424,552},{432,5... | collective-permute-start | bytes 19976 | tf_op jit(solution)/shard_map/ppermute | solution.py:337
  32.9 5.3 %collective-permute-start.6 = (f32[13,128]{1,0:T(8,128)S(1)}, f32[13,128]{1,0:T(8,128)S(1)}, u32[]{:S(2)}, u32[]{:S(2)}) collective-permute-start(f32[13,128]{1,0:T(8,128)S(1)} %get-tuple-element.43.message_ref), channel_id=1, source_target_pairs={{512,640},{520,648},{528,656},{536,664},{544,672},{552,680},{560,6... | collective-permute-start | bytes 19976 | tf_op jit(solution)/shard_map/ppermute | solution.py:337
  34.2 8.3 %collective-permute-start.5 = (f32[13,128]{1,0:T(8,128)S(1)}, f32[13,128]{1,0:T(8,128)S(1)}, u32[]{:S(2)}, u32[]{:S(2)}) collective-permute-start(f32[13,128]{1,0:T(8,128)S(1)} %get-tuple-element.43.message_ref), channel_id=1, source_target_pairs={{512,768},{520,776},{528,784},{536,792},{544,800},{552,808},{560,8... | collective-permute-start | bytes 19976 | tf_op jit(solution)/shard_map/ppermute | solution.py:337
  35.5 11.0 %collective-permute-start.4 = (f32[13,128]{1,0:T(8,128)S(1)}, f32[13,128]{1,0:T(8,128)S(1)}, u32[]{:S(2)}, u32[]{:S(2)}) collective-permute-start(f32[13,128]{1,0:T(8,128)S(1)} %get-tuple-element.43.message_ref), channel_id=1, source_target_pairs={{512,896},{520,904},{528,912},{536,920},{544,928},{552,936},{560,9... | collective-permute-start | bytes 19976 | tf_op jit(solution)/shard_map/ppermute | solution.py:337
  47.2 15.5 %all-to-all-start.2 = ((f32[16,1,1408]{2,1,0:T(1,128)}), f32[16,1,1408]{2,1,0:T(1,128)S(1)}, u32[]{:S(2)}, u32[]{:S(2)}) async-start(f32[16,1,1408]{2,1,0:T(1,128)} %bitcast.4), calls=%async_computation.2 | async-start | bytes 180224 | tf_op jit(solution)/shard_map/all_to_all | solution.py:330

commit v3 on v2

--- a/solution.py
+++ b/solution.py
@@ -21,6 +21,7 @@
 RUNS = 8
 CHAIN = 5
 JUMPS = (3, 2, 1)
+PIECES = 4
 F32 = jnp.float32
 
 
@@ -275,7 +276,7 @@
             run = run + first
 
 
-def output_kernel(start_ref, product_ref, query_ref, edge_ref, local_ref, decay_ref, residue_ref, out_ref, wide_ref):
+def output_kernel(start_ref, product_ref, query_ref, edge_ref, local_ref, decay_ref, residue_ref, out, wide_ref, out_v, sems):
     blocks = SUB
     span = SUB * blocks
     rows = product_ref.shape[0] // blocks
@@ -307,12 +308,21 @@
 
     for s in range(TAPS - 1, SUB):
         terms = token(0, s, terms)
-    lax.fori_loop(1, rows // SUB, step, tuple(terms))
-    for pair in range(rows // (2 * SUB)):
-        for j in range(blocks):
-            base = 2 * pair * span + j * SUB
-            both = jnp.concatenate([wide_ref[pl.ds(base, SUB), :], wide_ref[pl.ds(base + span, SUB), :]], 0)
-            out_ref[pair * 2 * SUB : (pair + 1) * 2 * SUB, j * LANES : (j + 1) * LANES] = both.astype(jnp.bfloat16)
+    size = rows // PIECES
+    copies = []
+    for piece in range(PIECES):
+        first, end = piece * size // SUB, (piece + 1) * size // SUB
+        terms = lax.fori_loop(max(first, 1), end, step, tuple(terms))
+        for pair in range(first // 2, end // 2):
+            for j in range(blocks):
+                base = 2 * pair * span + j * SUB
+                both = jnp.concatenate([wide_ref[pl.ds(base, SUB), :], wide_ref[pl.ds(base + span, SUB), :]], 0)
+                out_v[pair * 2 * SUB : (pair + 1) * 2 * SUB, j * LANES : (j + 1) * LANES] = both.astype(out_v.dtype)
+        part = pl.ds(piece * size, size)
+        copies.append(pltpu.make_async_copy(out_v.at[part, :], out.at[part, :], sems.at[piece]))
+        copies[-1].start()
+    for copy in copies:
+        copy.wait()
 
 
 def shape(*dims):
@@ -410,12 +420,19 @@
         spread_kernel(message_ref, heard_ref, refs[: len(jumps)], *refs[len(jumps) :])
 
     starts = call(spread, shape(run * BACK, LANES), (message, heard, *jumps, powers, prefix, halos))
-    return call(
+    inputs = (exchange(starts, near), product, query, edges, local, decay, gain)
+    return pl.pallas_call(
         output_kernel,
-        jax.ShapeDtypeStruct((rows, chans), jnp.bfloat16),
-        (exchange(starts, near), product, query, edges, local, decay, gain),
-        (pltpu.VMEM((rows * blocks, LANES), F32),),
-    )
+        in_specs=[pl.BlockSpec(memory_space=pltpu.VMEM)] * len(inputs),
+        out_specs=pl.BlockSpec(memory_space=pl.ANY),
+        out_shape=jax.ShapeDtypeStruct((rows, chans), jnp.bfloat16),
+        scratch_shapes=[
+            pltpu.VMEM((rows * blocks, LANES), F32),
+            pltpu.VMEM((rows, chans), jnp.bfloat16),
+            pltpu.SemaphoreType.DMA((PIECES,)),
+        ],
+        name="output",
+    )(*[vmem(x) for x in inputs])
 
 
 def solution(mesh):

time: 64.6 us -> 64.6 us (level)
    pallas_call x9 -> x8, Pallas kernels: 3.98 us -> 2.49 us  [call(): pl.pallas_call(kernel, out_shape=out_shape, scratch_shapes=list(scratch))]
    pallas_call x0 -> x1, Pallas kernels: none -> 1.47 us  [block(): pl.pallas_call(output_kernel, in_specs=[pl.BlockSpec(memory_space=pltpu.V...]
where the time goes in v3:
time: 64.6 us; the launch traced here: 64.2 us
  blocking collectives  27.2 us (42%)
  waiting for transfers between devices  16.7 us (26%)
  starting transfers between devices  13.6 us (21%)
  Pallas kernels  6.56 us (10%)
    all_to_all x1, blocking collectives, exchange(): lax.all_to_all(flat, 'ctx', split_axis=0, concat_axis=0, tiled=True, axis...  17.3 us
    all_to_all x1, blocking collectives, block(): lax.all_to_all(packed, 'dp', split_axis=0, concat_axis=0, tiled=True)  9.87 us
    ppermute x7, waiting for transfers between devices, send(): return lax.ppermute(value, 'ctx', pairs)  9.71 us
    all_to_all x1, starting transfers between devices, exchange(): lax.all_to_all(flat, 'ctx', split_axis=0, concat_axis=0, tiled=True, axis...  7.16 us
    all_to_all x1, waiting for transfers between devices, exchange(): lax.all_to_all(flat, 'ctx', split_axis=0, concat_axis=0, tiled=True, axis...  6.95 us
    ppermute x7, starting transfers between devices, send(): return lax.ppermute(value, 'ctx', pairs)  6.48 us
    pallas_call x8, Pallas kernels, call(): pl.pallas_call(kernel, out_shape=out_shape, scratch_shapes=list(scratch))  2.49 us
    pallas_call x1, Pallas kernels, block(): pl.pallas_call(output_kernel, in_specs=[pl.BlockSpec(memory_space=pltpu.V...  1.47 us
  transfers between devices with their start and end apart: 8, of which 4 were waited for; matrix products, arithmetic and copies ran while one was open for 0% of the time, Pallas kernels for 2%

profile of v3, /device:TPU:897, one launch (start us, length us, event | category | flops | bytes accessed | tf_op | source)
XLA Modules:
  0.0 64.2 jit_solution(10839356760891534771)
XLA Ops:
  0.0 1.2 %pack.1 = (f32[8,2,128]{2,1,0:T(2,128)S(1)}, bf16[3,128,1024]{2,1,0:T(8,128)(2,1)S(1)}, f32[72,128]{1,0:T(8,128)S(1)}) custom-call(bf16[3,128,1024]{2,1,0:T(8,128)(2,1)} %stream.3, f32[3,3,8192]{2,1,0:T(4,128)} %taps.1, f32[2,512]{1,0:T(2,128)} %rates.1, f32[2,512]{1,0:T(2,128)} %residues.1), custom_call_target="tpu_custom_call" | custom-call | tf_op jit(solution)/shard_map/pack/pallas_call | solution.py:363
  1.2 9.9 %all_to_all.15 = f32[8,2,128]{2,1,0:T(2,128)S(1)} all-to-all(f32[8,2,128]{2,1,0:T(2,128)S(1)} %get-tuple-element.30), channel_id=1, replica_groups=mesh['ctx'=128,'dp'=8] {'dp'}, dimensions={0} | all-to-all | bytes 16384 | tf_op jit(solution)/shard_map/all_to_all | solution.py:379
  11.1 0.4 shard_map.46
  11.5 0.9 %shard_map.47 = (f32[208,128]{1,0:T(8,128)S(1)}, f32[128,128]{1,0:T(8,128)S(1)}, f32[128,128]{1,0:T(8,128)S(1)}, f32[128,128]{1,0:T(8,128)S(1)}) custom-call(f32[1024,128]{1,0:T(8,128)S(1)} %get-tuple-element.31.product_ref, f32[16,128]{1,0:T(8,128)S(1)} %bitcast.10, f32[80,128]{1,0:T(8,128)S(1)} %get-tuple-element.32.edge_ref), custom_call_target="tpu_custom_call" | custom-call | tf_op jit(solution)/shard_map/pallas_call | solution.py:333
  12.4 17.3 %all_to_all.16 = f32[16,1,1664]{2,1,0:T(1,128)S(1)} all-to-all(f32[16,1,1664]{2,1,0:T(1,128)S(1)} %bitcast.8), channel_id=1, replica_groups={{0,8,16,24,32,40,48,56,64,72,80,88,96,104,112,120},{128,136,144,152,160..., dimensions={0} | all-to-all | bytes 212992 | tf_op jit(solution)/shard_map/all_to_all | solution.py:340
  29.8 0.1 shard_map.48
  29.9 0.7 %collective-permute-start = (f32[13,128]{1,0:T(8,128)S(1)}, f32[13,128]{1,0:T(8,128)S(1)}, u32[]{:S(2)}, u32[]{:S(2)}) collective-permute-start(f32[13,128]{1,0:T(8,128)S(1)} %get-tuple-element.35.message_ref.after_ref), channel_id=1, source_target_pairs={{0,128},{8,136},{16,144},{24,152},{32,160},{40,168},{48,176},{56,1... | collective-permute-start | bytes 19976 | tf_op jit(solution)/shard_map/ppermute | solution.py:347
  30.5 0.0 collective-permute-done.got_ref
  30.6 0.1 shard_map.49
  30.6 0.7 %collective-permute-start.1 = (f32[13,128]{1,0:T(8,128)S(1)}, f32[13,128]{1,0:T(8,128)S(1)}, u32[]{:S(2)}, u32[]{:S(2)}) collective-permute-start(f32[13,128]{1,0:T(8,128)S(1)} %get-tuple-element.37.message_ref), channel_id=1, source_target_pairs={{128,256},{136,264},{144,272},{152,280},{160,288},{168,296},{176,3... | collective-permute-start | bytes 19976 | tf_op jit(solution)/shard_map/ppermute | solution.py:347
  31.3 0.0 collective-permute-done.1.got_ref
  31.3 0.1 shard_map.50
  31.4 0.7 %collective-permute-start.2 = (f32[13,128]{1,0:T(8,128)S(1)}, f32[13,128]{1,0:T(8,128)S(1)}, u32[]{:S(2)}, u32[]{:S(2)}) collective-permute-start(f32[13,128]{1,0:T(8,128)S(1)} %get-tuple-element.39.message_ref), channel_id=1, source_target_pairs={{256,384},{264,392},{272,400},{280,408},{288,416},{296,424},{304,4... | collective-permute-start | bytes 19976 | tf_op jit(solution)/shard_map/ppermute | solution.py:347
  32.0 0.0 collective-permute-done.2.got_ref
  32.1 0.1 shard_map.51
  32.1 0.7 %collective-permute-start.3 = (f32[13,128]{1,0:T(8,128)S(1)}, f32[13,128]{1,0:T(8,128)S(1)}, u32[]{:S(2)}, u32[]{:S(2)}) collective-permute-start(f32[13,128]{1,0:T(8,128)S(1)} %get-tuple-element.41.message_ref), channel_id=1, source_target_pairs={{384,512},{392,520},{400,528},{408,536},{416,544},{424,552},{432,5... | collective-permute-start | bytes 19976 | tf_op jit(solution)/shard_map/ppermute | solution.py:347
  32.8 0.0 collective-permute-done.3.got_ref
  32.8 0.1 shard_map.52
  32.9 1.3 %collective-permute-start.6 = (f32[13,128]{1,0:T(8,128)S(1)}, f32[13,128]{1,0:T(8,128)S(1)}, u32[]{:S(2)}, u32[]{:S(2)}) collective-permute-start(f32[13,128]{1,0:T(8,128)S(1)} %get-tuple-element.43.message_ref), channel_id=1, source_target_pairs={{512,640},{520,648},{528,656},{536,664},{544,672},{552,680},{560,6... | collective-permute-start | bytes 19976 | tf_op jit(solution)/shard_map/ppermute | solution.py:347
  34.2 1.3 %collective-permute-start.5 = (f32[13,128]{1,0:T(8,128)S(1)}, f32[13,128]{1,0:T(8,128)S(1)}, u32[]{:S(2)}, u32[]{:S(2)}) collective-permute-start(f32[13,128]{1,0:T(8,128)S(1)} %get-tuple-element.43.message_ref), channel_id=1, source_target_pairs={{512,768},{520,776},{528,784},{536,792},{544,800},{552,808},{560,8... | collective-permute-start | bytes 19976 | tf_op jit(solution)/shard_map/ppermute | solution.py:347
  35.5 1.3 %collective-permute-start.4 = (f32[13,128]{1,0:T(8,128)S(1)}, f32[13,128]{1,0:T(8,128)S(1)}, u32[]{:S(2)}, u32[]{:S(2)}) collective-permute-start(f32[13,128]{1,0:T(8,128)S(1)} %get-tuple-element.43.message_ref), channel_id=1, source_target_pairs={{512,896},{520,904},{528,912},{536,920},{544,928},{552,936},{560,9... | collective-permute-start | bytes 19976 | tf_op jit(solution)/shard_map/ppermute | solution.py:347
  36.8 1.4 %collective-permute-done.6.refs_2_ = f32[13,128]{1,0:T(8,128)S(1)} collective-permute-done((f32[13,128]{1,0:T(8,128)S(1)}, f32[13,128]{1,0:T(8,128)S(1)}, u32[]{:S(2)}, u32[]{:S(2)}) %collective-permute-start.6) | collective-permute-done | bytes 6688 | tf_op jit(solution)/shard_map/ppermute | solution.py:347
  38.2 4.3 %collective-permute-done.5.refs_1_ = f32[13,128]{1,0:T(8,128)S(1)} collective-permute-done((f32[13,128]{1,0:T(8,128)S(1)}, f32[13,128]{1,0:T(8,128)S(1)}, u32[]{:S(2)}, u32[]{:S(2)}) %collective-permute-start.5) | collective-permute-done | bytes 6688 | tf_op jit(solution)/shard_map/ppermute | solution.py:347
  42.5 4.0 %collective-permute-done.4.refs_0_ = f32[13,128]{1,0:T(8,128)S(1)} collective-permute-done((f32[13,128]{1,0:T(8,128)S(1)}, f32[13,128]{1,0:T(8,128)S(1)}, u32[]{:S(2)}, u32[]{:S(2)}) %collective-permute-start.4) | collective-permute-done | bytes 6688 | tf_op jit(solution)/shard_map/ppermute | solution.py:347
  46.5 0.8 %shard_map.53 = f32[176,128]{1,0:T(8,128)} custom-call(f32[13,128]{1,0:T(8,128)S(1)} %get-tuple-element.43.message_ref, f32[13,128]{1,0:T(8,128)S(1)} %get-tuple-element.44.heard_ref, f32[13,128]{1,0:T(8,128)S(1)} %collective-permute-done.4.refs_0_, f32[13,128]{1,0:T(8,128)S(1)} %collective-permute-done.5.refs_1_, ...), custom_call_target="tpu_custom_call" | custom-call | tf_op jit(solution)/shard_map/pallas_call | solution.py:333
  47.2 7.2 %all-to-all-start.2 = ((f32[16,1,1408]{2,1,0:T(1,128)}), f32[16,1,1408]{2,1,0:T(1,128)S(1)}, u32[]{:S(2)}, u32[]{:S(2)}) async-start(f32[16,1,1408]{2,1,0:T(1,128)} %bitcast.4), calls=%async_computation.2 | async-start | bytes 180224 | tf_op jit(solution)/shard_map/all_to_all | solution.py:340
  54.4 1.4 %local.1 = (f32[1024,128]{1,0:T(8,128)S(1)}, f32[1024,128]{1,0:T(8,128)S(1)}) custom-call(f32[1024,128]{1,0:T(8,128)S(1)} %get-tuple-element.31.product_ref, f32[128,128]{1,0:T(8,128)S(1)} %get-tuple-element.47.decay_ref, f32[128,128]{1,0:T(8,128)S(1)} %get-tuple-element.48.residue_ref, f32[72,128]{1,0:T(8,128)S(1)} %get-tuple-element.29.taps_ref, ...), custom_call_target="tpu_custom_call" | custom-call | tf_op jit(solution)/shard_map/local/pallas_call | solution.py:406
  55.8 6.9 %all-to-all-done.2 = f32[16,1,1408]{2,1,0:T(1,128)S(1)} async-done(((f32[16,1,1408]{2,1,0:T(1,128)}), f32[16,1,1408]{2,1,0:T(1,128)S(1)}, u32[]{:S(2)}, u32[]{:S(2)}) %all-to-all-start.2) | async-done | bytes 90144 | tf_op jit(solution)/shard_map/all_to_all | solution.py:340
  62.7 1.5 %output.1 = bf16[128,1024]{1,0:T(8,128)(2,1)} custom-call(f32[176,128]{1,0:T(8,128)S(1)} %bitcast.7, f32[1024,128]{1,0:T(8,128)S(1)} %get-tuple-element.31.product_ref, f32[1024,128]{1,0:T(8,128)S(1)} %get-tuple-element.49.query_ref, f32[80,128]{1,0:T(8,128)S(1)} %get-tuple-element.32.edge_ref, f32[1024,128]{1,0:T(8,128)S(1)} %get-tuple-element.50.local_ref, ...), custom_call_target="tpu_custom_call" | custom-call | tf_op jit(solution)/shard_map/output/pallas_call | solution.py:424
  (1 shorter events, 0.0 us)
Async XLA Ops:
  29.9 0.7 %collective-permute-start = (f32[13,128]{1,0:T(8,128)S(1)}, f32[13,128]{1,0:T(8,128)S(1)}, u32[]{:S(2)}, u32[]{:S(2)}) collective-permute-start(f32[13,128]{1,0:T(8,128)S(1)} %get-tuple-element.35.message_ref.after_ref), channel_id=1, source_target_pairs={{0,128},{8,136},{16,144},{24,152},{32,160},{40,168},{48,176},{56,1... | collective-permute-start | bytes 19976 | tf_op jit(solution)/shard_map/ppermute | solution.py:347
  30.6 0.7 %collective-permute-start.1 = (f32[13,128]{1,0:T(8,128)S(1)}, f32[13,128]{1,0:T(8,128)S(1)}, u32[]{:S(2)}, u32[]{:S(2)}) collective-permute-start(f32[13,128]{1,0:T(8,128)S(1)} %get-tuple-element.37.message_ref), channel_id=1, source_target_pairs={{128,256},{136,264},{144,272},{152,280},{160,288},{168,296},{176,3... | collective-permute-start | bytes 19976 | tf_op jit(solution)/shard_map/ppermute | solution.py:347
  31.4 0.7 %collective-permute-start.2 = (f32[13,128]{1,0:T(8,128)S(1)}, f32[13,128]{1,0:T(8,128)S(1)}, u32[]{:S(2)}, u32[]{:S(2)}) collective-permute-start(f32[13,128]{1,0:T(8,128)S(1)} %get-tuple-element.39.message_ref), channel_id=1, source_target_pairs={{256,384},{264,392},{272,400},{280,408},{288,416},{296,424},{304,4... | collective-permute-start | bytes 19976 | tf_op jit(solution)/shard_map/ppermute | solution.py:347
  32.1 0.7 %collective-permute-start.3 = (f32[13,128]{1,0:T(8,128)S(1)}, f32[13,128]{1,0:T(8,128)S(1)}, u32[]{:S(2)}, u32[]{:S(2)}) collective-permute-start(f32[13,128]{1,0:T(8,128)S(1)} %get-tuple-element.41.message_ref), channel_id=1, source_target_pairs={{384,512},{392,520},{400,528},{408,536},{416,544},{424,552},{432,5... | collective-permute-start | bytes 19976 | tf_op jit(solution)/shard_map/ppermute | solution.py:347
  32.9 5.3 %collective-permute-start.6 = (f32[13,128]{1,0:T(8,128)S(1)}, f32[13,128]{1,0:T(8,128)S(1)}, u32[]{:S(2)}, u32[]{:S(2)}) collective-permute-start(f32[13,128]{1,0:T(8,128)S(1)} %get-tuple-element.43.message_ref), channel_id=1, source_target_pairs={{512,640},{520,648},{528,656},{536,664},{544,672},{552,680},{560,6... | collective-permute-start | bytes 19976 | tf_op jit(solution)/shard_map/ppermute | solution.py:347
  34.2 8.3 %collective-permute-start.5 = (f32[13,128]{1,0:T(8,128)S(1)}, f32[13,128]{1,0:T(8,128)S(1)}, u32[]{:S(2)}, u32[]{:S(2)}) collective-permute-start(f32[13,128]{1,0:T(8,128)S(1)} %get-tuple-element.43.message_ref), channel_id=1, source_target_pairs={{512,768},{520,776},{528,784},{536,792},{544,800},{552,808},{560,8... | collective-permute-start | bytes 19976 | tf_op jit(solution)/shard_map/ppermute | solution.py:347
  35.5 11.0 %collective-permute-start.4 = (f32[13,128]{1,0:T(8,128)S(1)}, f32[13,128]{1,0:T(8,128)S(1)}, u32[]{:S(2)}, u32[]{:S(2)}) collective-permute-start(f32[13,128]{1,0:T(8,128)S(1)} %get-tuple-element.43.message_ref), channel_id=1, source_target_pairs={{512,896},{520,904},{528,912},{536,920},{544,928},{552,936},{560,9... | collective-permute-start | bytes 19976 | tf_op jit(solution)/shard_map/ppermute | solution.py:347
  47.2 15.5 %all-to-all-start.2 = ((f32[16,1,1408]{2,1,0:T(1,128)}), f32[16,1,1408]{2,1,0:T(1,128)S(1)}, u32[]{:S(2)}, u32[]{:S(2)}) async-start(f32[16,1,1408]{2,1,0:T(1,128)} %bitcast.4), calls=%async_computation.2 | async-start | bytes 180224 | tf_op jit(solution)/shard_map/all_to_all | solution.py:340

commit v4 on v3

--- a/solution.py
+++ b/solution.py
@@ -20,7 +20,7 @@
 BACK = PART + 3
 RUNS = 8
 CHAIN = 5
-JUMPS = (3, 2, 1)
+JUMPS = (2, 3, 1)
 PIECES = 4
 F32 = jnp.float32
 
@@ -260,7 +260,7 @@
     index = lax.axis_index("ctx") // count
     run = heard_ref[:PART, :]
     halo = heard_ref[pl.ds(PART, EDGES), :]
-    for n, far in enumerate(JUMPS):
+    for n, far in enumerate(sorted(JUMPS, reverse=True)):
         source = index - far
         value = jumps_ref[n][:PART, :]
         edges = jumps_ref[n][pl.ds(PART, EDGES), :]
@@ -351,7 +351,8 @@
     for z in range(CHAIN - 1):
         got = send(message, [(z, z + 1)])
         message, heard = call(functools.partial(link_kernel, z, run), (row, row), (message, heard, got, powers))
-    jumps = [send(message, [(z, z + far) for z in range(CHAIN - 1, RUNS - far)]) for far in JUMPS]
+    got = {far: send(message, [(z, z + far) for z in range(CHAIN - 1, RUNS - far)]) for far in JUMPS}
+    jumps = [got[far] for far in sorted(JUMPS, reverse=True)]
     return message, heard, jumps
 
 

time: 64.6 us -> 64.6 us (level)
  no operation moved by 1% of the time
where the time goes in v4:
time: 64.6 us; the launch traced here: 64.2 us
  blocking collectives  27.2 us (42%)
  waiting for transfers between devices  16.7 us (26%)
  starting transfers between devices  13.6 us (21%)
  Pallas kernels  6.56 us (10%)
    all_to_all x1, blocking collectives, exchange(): lax.all_to_all(flat, 'ctx', split_axis=0, concat_axis=0, tiled=True, axis...  17.3 us
    all_to_all x1, blocking collectives, block(): lax.all_to_all(packed, 'dp', split_axis=0, concat_axis=0, tiled=True)  9.87 us
    ppermute x7, waiting for transfers between devices, send(): return lax.ppermute(value, 'ctx', pairs)  9.71 us
    all_to_all x1, starting transfers between devices, exchange(): lax.all_to_all(flat, 'ctx', split_axis=0, concat_axis=0, tiled=True, axis...  7.16 us
    all_to_all x1, waiting for transfers between devices, exchange(): lax.all_to_all(flat, 'ctx', split_axis=0, concat_axis=0, tiled=True, axis...  6.95 us
    ppermute x7, starting transfers between devices, send(): return lax.ppermute(value, 'ctx', pairs)  6.48 us
    pallas_call x8, Pallas kernels, call(): pl.pallas_call(kernel, out_shape=out_shape, scratch_shapes=list(scratch))  2.49 us
    pallas_call x1, Pallas kernels, block(): pl.pallas_call(output_kernel, in_specs=[pl.BlockSpec(memory_space=pltpu.V...  1.47 us
  transfers between devices with their start and end apart: 8, of which 4 were waited for; matrix products, arithmetic and copies ran while one was open for 0% of the time, Pallas kernels for 2%

profile of v4, /device:TPU:897, one launch (start us, length us, event | category | flops | bytes accessed | tf_op | source)
XLA Modules:
  0.0 64.2 jit_solution(10839356760891534771)
XLA Ops:
  0.0 1.2 %pack.1 = (f32[8,2,128]{2,1,0:T(2,128)S(1)}, bf16[3,128,1024]{2,1,0:T(8,128)(2,1)S(1)}, f32[72,128]{1,0:T(8,128)S(1)}) custom-call(bf16[3,128,1024]{2,1,0:T(8,128)(2,1)} %stream.3, f32[3,3,8192]{2,1,0:T(4,128)} %taps.1, f32[2,512]{1,0:T(2,128)} %rates.1, f32[2,512]{1,0:T(2,128)} %residues.1), custom_call_target="tpu_custom_call" | custom-call | tf_op jit(solution)/shard_map/pack/pallas_call | solution.py:364
  1.2 9.9 %all_to_all.15 = f32[8,2,128]{2,1,0:T(2,128)S(1)} all-to-all(f32[8,2,128]{2,1,0:T(2,128)S(1)} %get-tuple-element.30), channel_id=1, replica_groups=mesh['ctx'=128,'dp'=8] {'dp'}, dimensions={0} | all-to-all | bytes 16384 | tf_op jit(solution)/shard_map/all_to_all | solution.py:380
  11.1 0.4 shard_map.46
  11.5 0.9 %shard_map.47 = (f32[208,128]{1,0:T(8,128)S(1)}, f32[128,128]{1,0:T(8,128)S(1)}, f32[128,128]{1,0:T(8,128)S(1)}, f32[128,128]{1,0:T(8,128)S(1)}) custom-call(f32[1024,128]{1,0:T(8,128)S(1)} %get-tuple-element.31.product_ref, f32[16,128]{1,0:T(8,128)S(1)} %bitcast.10, f32[80,128]{1,0:T(8,128)S(1)} %get-tuple-element.32.edge_ref), custom_call_target="tpu_custom_call" | custom-call | tf_op jit(solution)/shard_map/pallas_call | solution.py:333
  12.4 17.3 %all_to_all.16 = f32[16,1,1664]{2,1,0:T(1,128)S(1)} all-to-all(f32[16,1,1664]{2,1,0:T(1,128)S(1)} %bitcast.8), channel_id=1, replica_groups={{0,8,16,24,32,40,48,56,64,72,80,88,96,104,112,120},{128,136,144,152,160..., dimensions={0} | all-to-all | bytes 212992 | tf_op jit(solution)/shard_map/all_to_all | solution.py:340
  29.8 0.1 shard_map.48
  29.9 0.7 %collective-permute-start = (f32[13,128]{1,0:T(8,128)S(1)}, f32[13,128]{1,0:T(8,128)S(1)}, u32[]{:S(2)}, u32[]{:S(2)}) collective-permute-start(f32[13,128]{1,0:T(8,128)S(1)} %get-tuple-element.35.message_ref.after_ref), channel_id=1, source_target_pairs={{0,128},{8,136},{16,144},{24,152},{32,160},{40,168},{48,176},{56,1... | collective-permute-start | bytes 19976 | tf_op jit(solution)/shard_map/ppermute | solution.py:347
  30.5 0.0 collective-permute-done.got_ref
  30.6 0.1 shard_map.49
  30.6 0.7 %collective-permute-start.1 = (f32[13,128]{1,0:T(8,128)S(1)}, f32[13,128]{1,0:T(8,128)S(1)}, u32[]{:S(2)}, u32[]{:S(2)}) collective-permute-start(f32[13,128]{1,0:T(8,128)S(1)} %get-tuple-element.37.message_ref), channel_id=1, source_target_pairs={{128,256},{136,264},{144,272},{152,280},{160,288},{168,296},{176,3... | collective-permute-start | bytes 19976 | tf_op jit(solution)/shard_map/ppermute | solution.py:347
  31.3 0.0 collective-permute-done.1.got_ref
  31.3 0.1 shard_map.50
  31.4 0.7 %collective-permute-start.2 = (f32[13,128]{1,0:T(8,128)S(1)}, f32[13,128]{1,0:T(8,128)S(1)}, u32[]{:S(2)}, u32[]{:S(2)}) collective-permute-start(f32[13,128]{1,0:T(8,128)S(1)} %get-tuple-element.39.message_ref), channel_id=1, source_target_pairs={{256,384},{264,392},{272,400},{280,408},{288,416},{296,424},{304,4... | collective-permute-start | bytes 19976 | tf_op jit(solution)/shard_map/ppermute | solution.py:347
  32.0 0.0 collective-permute-done.2.got_ref
  32.1 0.1 shard_map.51
  32.1 0.7 %collective-permute-start.3 = (f32[13,128]{1,0:T(8,128)S(1)}, f32[13,128]{1,0:T(8,128)S(1)}, u32[]{:S(2)}, u32[]{:S(2)}) collective-permute-start(f32[13,128]{1,0:T(8,128)S(1)} %get-tuple-element.41.message_ref), channel_id=1, source_target_pairs={{384,512},{392,520},{400,528},{408,536},{416,544},{424,552},{432,5... | collective-permute-start | bytes 19976 | tf_op jit(solution)/shard_map/ppermute | solution.py:347
  32.8 0.0 collective-permute-done.3.got_ref
  32.8 0.1 shard_map.52
  32.9 1.3 %collective-permute-start.6 = (f32[13,128]{1,0:T(8,128)S(1)}, f32[13,128]{1,0:T(8,128)S(1)}, u32[]{:S(2)}, u32[]{:S(2)}) collective-permute-start(f32[13,128]{1,0:T(8,128)S(1)} %get-tuple-element.43.message_ref), channel_id=1, source_target_pairs={{512,640},{520,648},{528,656},{536,664},{544,672},{552,680},{560,6... | collective-permute-start | bytes 19976 | tf_op jit(solution)/shard_map/ppermute | solution.py:347
  34.2 1.3 %collective-permute-start.5 = (f32[13,128]{1,0:T(8,128)S(1)}, f32[13,128]{1,0:T(8,128)S(1)}, u32[]{:S(2)}, u32[]{:S(2)}) collective-permute-start(f32[13,128]{1,0:T(8,128)S(1)} %get-tuple-element.43.message_ref), channel_id=1, source_target_pairs={{512,768},{520,776},{528,784},{536,792},{544,800},{552,808},{560,8... | collective-permute-start | bytes 19976 | tf_op jit(solution)/shard_map/ppermute | solution.py:347
  35.5 1.3 %collective-permute-start.4 = (f32[13,128]{1,0:T(8,128)S(1)}, f32[13,128]{1,0:T(8,128)S(1)}, u32[]{:S(2)}, u32[]{:S(2)}) collective-permute-start(f32[13,128]{1,0:T(8,128)S(1)} %get-tuple-element.43.message_ref), channel_id=1, source_target_pairs={{512,896},{520,904},{528,912},{536,920},{544,928},{552,936},{560,9... | collective-permute-start | bytes 19976 | tf_op jit(solution)/shard_map/ppermute | solution.py:347
  36.8 1.4 %collective-permute-done.6.refs_2_ = f32[13,128]{1,0:T(8,128)S(1)} collective-permute-done((f32[13,128]{1,0:T(8,128)S(1)}, f32[13,128]{1,0:T(8,128)S(1)}, u32[]{:S(2)}, u32[]{:S(2)}) %collective-permute-start.6) | collective-permute-done | bytes 6688 | tf_op jit(solution)/shard_map/ppermute | solution.py:347
  38.2 4.3 %collective-permute-done.5.refs_1_ = f32[13,128]{1,0:T(8,128)S(1)} collective-permute-done((f32[13,128]{1,0:T(8,128)S(1)}, f32[13,128]{1,0:T(8,128)S(1)}, u32[]{:S(2)}, u32[]{:S(2)}) %collective-permute-start.5) | collective-permute-done | bytes 6688 | tf_op jit(solution)/shard_map/ppermute | solution.py:347
  42.5 4.0 %collective-permute-done.4.refs_0_ = f32[13,128]{1,0:T(8,128)S(1)} collective-permute-done((f32[13,128]{1,0:T(8,128)S(1)}, f32[13,128]{1,0:T(8,128)S(1)}, u32[]{:S(2)}, u32[]{:S(2)}) %collective-permute-start.4) | collective-permute-done | bytes 6688 | tf_op jit(solution)/shard_map/ppermute | solution.py:347
  46.5 0.8 %shard_map.53 = f32[176,128]{1,0:T(8,128)} custom-call(f32[13,128]{1,0:T(8,128)S(1)} %get-tuple-element.43.message_ref, f32[13,128]{1,0:T(8,128)S(1)} %get-tuple-element.44.heard_ref, f32[13,128]{1,0:T(8,128)S(1)} %collective-permute-done.4.refs_0_, f32[13,128]{1,0:T(8,128)S(1)} %collective-permute-done.5.refs_1_, ...), custom_call_target="tpu_custom_call" | custom-call | tf_op jit(solution)/shard_map/pallas_call | solution.py:333
  47.2 7.2 %all-to-all-start.2 = ((f32[16,1,1408]{2,1,0:T(1,128)}), f32[16,1,1408]{2,1,0:T(1,128)S(1)}, u32[]{:S(2)}, u32[]{:S(2)}) async-start(f32[16,1,1408]{2,1,0:T(1,128)} %bitcast.4), calls=%async_computation.2 | async-start | bytes 180224 | tf_op jit(solution)/shard_map/all_to_all | solution.py:340
  54.4 1.4 %local.1 = (f32[1024,128]{1,0:T(8,128)S(1)}, f32[1024,128]{1,0:T(8,128)S(1)}) custom-call(f32[1024,128]{1,0:T(8,128)S(1)} %get-tuple-element.31.product_ref, f32[128,128]{1,0:T(8,128)S(1)} %get-tuple-element.47.decay_ref, f32[128,128]{1,0:T(8,128)S(1)} %get-tuple-element.48.residue_ref, f32[72,128]{1,0:T(8,128)S(1)} %get-tuple-element.29.taps_ref, ...), custom_call_target="tpu_custom_call" | custom-call | tf_op jit(solution)/shard_map/local/pallas_call | solution.py:407
  55.8 6.9 %all-to-all-done.2 = f32[16,1,1408]{2,1,0:T(1,128)S(1)} async-done(((f32[16,1,1408]{2,1,0:T(1,128)}), f32[16,1,1408]{2,1,0:T(1,128)S(1)}, u32[]{:S(2)}, u32[]{:S(2)}) %all-to-all-start.2) | async-done | bytes 90144 | tf_op jit(solution)/shard_map/all_to_all | solution.py:340
  62.7 1.5 %output.1 = bf16[128,1024]{1,0:T(8,128)(2,1)} custom-call(f32[176,128]{1,0:T(8,128)S(1)} %bitcast.7, f32[1024,128]{1,0:T(8,128)S(1)} %get-tuple-element.31.product_ref, f32[1024,128]{1,0:T(8,128)S(1)} %get-tuple-element.49.query_ref, f32[80,128]{1,0:T(8,128)S(1)} %get-tuple-element.32.edge_ref, f32[1024,128]{1,0:T(8,128)S(1)} %get-tuple-element.50.local_ref, ...), custom_call_target="tpu_custom_call" | custom-call | tf_op jit(solution)/shard_map/output/pallas_call | solution.py:425
  (1 shorter events, 0.0 us)
Async XLA Ops:
  29.9 0.7 %collective-permute-start = (f32[13,128]{1,0:T(8,128)S(1)}, f32[13,128]{1,0:T(8,128)S(1)}, u32[]{:S(2)}, u32[]{:S(2)}) collective-permute-start(f32[13,128]{1,0:T(8,128)S(1)} %get-tuple-element.35.message_ref.after_ref), channel_id=1, source_target_pairs={{0,128},{8,136},{16,144},{24,152},{32,160},{40,168},{48,176},{56,1... | collective-permute-start | bytes 19976 | tf_op jit(solution)/shard_map/ppermute | solution.py:347
  30.6 0.7 %collective-permute-start.1 = (f32[13,128]{1,0:T(8,128)S(1)}, f32[13,128]{1,0:T(8,128)S(1)}, u32[]{:S(2)}, u32[]{:S(2)}) collective-permute-start(f32[13,128]{1,0:T(8,128)S(1)} %get-tuple-element.37.message_ref), channel_id=1, source_target_pairs={{128,256},{136,264},{144,272},{152,280},{160,288},{168,296},{176,3... | collective-permute-start | bytes 19976 | tf_op jit(solution)/shard_map/ppermute | solution.py:347
  31.4 0.7 %collective-permute-start.2 = (f32[13,128]{1,0:T(8,128)S(1)}, f32[13,128]{1,0:T(8,128)S(1)}, u32[]{:S(2)}, u32[]{:S(2)}) collective-permute-start(f32[13,128]{1,0:T(8,128)S(1)} %get-tuple-element.39.message_ref), channel_id=1, source_target_pairs={{256,384},{264,392},{272,400},{280,408},{288,416},{296,424},{304,4... | collective-permute-start | bytes 19976 | tf_op jit(solution)/shard_map/ppermute | solution.py:347
  32.1 0.7 %collective-permute-start.3 = (f32[13,128]{1,0:T(8,128)S(1)}, f32[13,128]{1,0:T(8,128)S(1)}, u32[]{:S(2)}, u32[]{:S(2)}) collective-permute-start(f32[13,128]{1,0:T(8,128)S(1)} %get-tuple-element.41.message_ref), channel_id=1, source_target_pairs={{384,512},{392,520},{400,528},{408,536},{416,544},{424,552},{432,5... | collective-permute-start | bytes 19976 | tf_op jit(solution)/shard_map/ppermute | solution.py:347
  32.9 5.3 %collective-permute-start.6 = (f32[13,128]{1,0:T(8,128)S(1)}, f32[13,128]{1,0:T(8,128)S(1)}, u32[]{:S(2)}, u32[]{:S(2)}) collective-permute-start(f32[13,128]{1,0:T(8,128)S(1)} %get-tuple-element.43.message_ref), channel_id=1, source_target_pairs={{512,640},{520,648},{528,656},{536,664},{544,672},{552,680},{560,6... | collective-permute-start | bytes 19976 | tf_op jit(solution)/shard_map/ppermute | solution.py:347
  34.2 8.3 %collective-permute-start.5 = (f32[13,128]{1,0:T(8,128)S(1)}, f32[13,128]{1,0:T(8,128)S(1)}, u32[]{:S(2)}, u32[]{:S(2)}) collective-permute-start(f32[13,128]{1,0:T(8,128)S(1)} %get-tuple-element.43.message_ref), channel_id=1, source_target_pairs={{512,768},{520,776},{528,784},{536,792},{544,800},{552,808},{560,8... | collective-permute-start | bytes 19976 | tf_op jit(solution)/shard_map/ppermute | solution.py:347
  35.5 11.0 %collective-permute-start.4 = (f32[13,128]{1,0:T(8,128)S(1)}, f32[13,128]{1,0:T(8,128)S(1)}, u32[]{:S(2)}, u32[]{:S(2)}) collective-permute-start(f32[13,128]{1,0:T(8,128)S(1)} %get-tuple-element.43.message_ref), channel_id=1, source_target_pairs={{512,896},{520,904},{528,912},{536,920},{544,928},{552,936},{560,9... | collective-permute-start | bytes 19976 | tf_op jit(solution)/shard_map/ppermute | solution.py:347
  47.2 15.5 %all-to-all-start.2 = ((f32[16,1,1408]{2,1,0:T(1,128)}), f32[16,1,1408]{2,1,0:T(1,128)S(1)}, u32[]{:S(2)}, u32[]{:S(2)}) async-start(f32[16,1,1408]{2,1,0:T(1,128)} %bitcast.4), calls=%async_computation.2 | async-start | bytes 180224 | tf_op jit(solution)/shard_map/all_to_all | solution.py:340
